TPU v7x, 32 devices: a whole 2x2x4 slice. The times are simulated.
32 devices in a mesh: occ: 8 (over z, x), aux: 4 (over y, core).
Axes of the slice: x: 2, y: 2, z: 4, core: 2. Of those that a mesh axis runs over, the one named last changes fastest.
Arguments:
- int_tiles: bfloat16 [32, 64, 128, 256], P('occ', 'aux'), may hold values from -0.5 to 0.5
- tile_ids: int32 [32, 64], P('occ', 'aux'), may hold values from 0 to 79, as said below
- tile_counts: int32 [32, 4], P('occ', 'aux'), may hold values from 8 to 16, as said below
- pair_list: int32 [64, 2], P('occ'), may hold values from 0 to 3
- occ_energy: float32 [32], replicated, may hold values from -2 to -0.5
- vir_energy: float32 [256], replicated, may hold values from 0.2 to 3
Outputs:
- gamma_tiles: bfloat16 [32, 64, 128, 256], P('occ', 'aux')
- density: float32 [256, 256], P('aux')
Inputs may be any that keep to these rules, and one draw needn't show every extreme that they name: `tile_ids`: within one orbital and one aux index's share the 16 tile numbers are distinct. Only the first tile_counts slots of a share are live; tiles and numbers of the others are never read. `pair_list`: column 0 indexes the asking occ index's orbitals, column 1 those of occ index r.
All inputs are finite; a program needn't handle non-finite values.
Results may differ from a plain program's by a relative error of at most 0.0085.
Values may be sent and summed in bfloat16 or wider, within the bound.
A program may use at most 256 MiB of HBM per device.

v0:
```python
import jax
import jax.numpy as jnp
from jax import lax
from jax.sharding import PartitionSpec as P


def amplitudes(coulomb, energy_pair, vir_energy):
    denominator = energy_pair[:, None, None] - vir_energy[None, :, None] - vir_energy[None, None, :]
    amplitude = coulomb / denominator
    return (amplitude, 2.0 * amplitude - jnp.swapaxes(amplitude, 1, 2))


def density_terms(amplitude_left, amplitude_right, spin_mixed):
    first_term = jnp.einsum(
        "rac,rbc->ab", amplitude_left, spin_mixed, precision=lax.Precision.HIGHEST
    )
    second_term = jnp.einsum(
        "rca,rcb->ab", amplitude_right, spin_mixed, precision=lax.Precision.HIGHEST
    )
    return first_term + second_term


def per_device(int_tiles, tile_ids, tile_counts, pair_list, occ_energy, vir_energy):
    peer_count = lax.axis_size("occ")
    group_count = lax.axis_size("aux")
    orb_count = int_tiles.shape[0]
    slot_count = int_tiles.shape[1]
    tile_rows = int_tiles.shape[2]
    virt_width = int_tiles.shape[3]
    pair_count = pair_list.shape[0]
    per_peer = pair_count // peer_count
    block_shape = (peer_count, per_peer, slot_count, tile_rows, virt_width)
    my_first = lax.axis_index("occ") * orb_count
    counts = tile_counts[:, 0]
    source = jnp.arange(pair_count, dtype=jnp.int32) // per_peer
    wanted = pair_list[:, 1]
    asked_for = lax.all_to_all(
        wanted.reshape(peer_count, per_peer), "occ", split_axis=0, concat_axis=0, tiled=True
    ).reshape(pair_count)
    arrived = (
        lax.all_to_all(
            int_tiles[asked_for].reshape(block_shape),
            "occ",
            split_axis=0,
            concat_axis=0,
            tiled=True,
        ),
        lax.all_to_all(
            tile_ids[asked_for].reshape(peer_count, per_peer, slot_count),
            "occ",
            split_axis=0,
            concat_axis=0,
            tiled=True,
        ),
        lax.all_to_all(
            counts[asked_for].reshape(peer_count, per_peer),
            "occ",
            split_axis=0,
            concat_axis=0,
            tiled=True,
        ),
    )
    here_index = pair_list[:, 0]
    there_global = source * orb_count + wanted
    there_tiles, there_ids, there_counts = arrived
    there_tiles = there_tiles.reshape(pair_count, slot_count, tile_rows, virt_width)
    there_ids = there_ids.reshape(pair_count, slot_count)
    there_counts = there_counts.reshape(pair_count)
    energy_pair = occ_energy[my_first + here_index] + occ_energy[there_global]
    slot_range = jnp.arange(slot_count, dtype=jnp.int32)

    def intersection_of(pair_index):
        here_orb = here_index[pair_index]
        here_live = slot_range < counts[here_orb]
        there_live = slot_range < there_counts[pair_index]
        same_tile = tile_ids[here_orb][:, None] == there_ids[pair_index][None, :]
        intersection = (same_tile & here_live[:, None] & there_live[None, :]).astype(jnp.bfloat16)
        return (int_tiles[here_orb], intersection)

    def rows_of_there(intersection, pair_index):
        return jnp.einsum(
            "st,tpb->spb", intersection, there_tiles[pair_index], preferred_element_type=jnp.float32
        ).astype(jnp.bfloat16)

    def coulomb_term(running, pair_index):
        here_block, intersection = intersection_of(pair_index)
        rows_there = rows_of_there(intersection, pair_index)
        term = lax.dot_general(
            here_block.reshape(-1, virt_width),
            rows_there.reshape(-1, virt_width),
            (((0,), (0,)), ((), ())),
            preferred_element_type=jnp.float32,
        )
        return (running, term)

    pair_range = jnp.arange(pair_count, dtype=jnp.int32)
    unused, partial_terms = lax.scan(coulomb_term, 0, pair_range)
    coulomb = lax.psum(partial_terms, "aux")
    amplitude, spin_mixed = amplitudes(coulomb, energy_pair, vir_energy)
    row_block = virt_width // group_count
    row_start = lax.axis_index("aux") * row_block
    amplitude_rows = lax.dynamic_slice_in_dim(amplitude, row_start, row_block, 1)
    amplitude_cols = lax.dynamic_slice_in_dim(amplitude, row_start, row_block, 2)
    density = density_terms(amplitude_rows, amplitude_cols, spin_mixed)
    weights = spin_mixed.astype(jnp.bfloat16)
    density = lax.psum(density.astype(jnp.bfloat16), "occ").astype(jnp.float32)
    part_shape = (slot_count, tile_rows, virt_width)

    def gamma_term(running, pair_index):
        here_block, intersection = intersection_of(pair_index)
        rows_there = rows_of_there(intersection, pair_index)
        rows_here = jnp.einsum(
            "st,spa->tpa", intersection, here_block, preferred_element_type=jnp.float32
        ).astype(jnp.bfloat16)
        pair_weights = weights[pair_index]
        here_part = lax.dot_general(
            rows_there.reshape(-1, virt_width),
            pair_weights,
            (((1,), (1,)), ((), ())),
            preferred_element_type=jnp.float32,
        )
        there_part = jnp.dot(
            rows_here.reshape(-1, virt_width), pair_weights, preferred_element_type=jnp.float32
        )
        return (
            running,
            (
                here_part.astype(jnp.bfloat16).reshape(part_shape),
                there_part.astype(jnp.bfloat16).reshape(part_shape),
            ),
        )

    unused, parts = lax.scan(gamma_term, 0, pair_range)
    here_parts, there_parts = parts
    returned = lax.all_to_all(
        there_parts.reshape(block_shape), "occ", split_axis=0, concat_axis=0, tiled=True
    ).reshape(pair_count, slot_count, tile_rows, virt_width)
    gamma_sum = jnp.zeros((orb_count, slot_count, tile_rows, virt_width), jnp.float32)
    gamma_sum = gamma_sum.at[here_index].add(here_parts.astype(jnp.float32))
    gamma_sum = gamma_sum.at[asked_for].add(returned.astype(jnp.float32))
    return (gamma_sum.astype(jnp.bfloat16), density)


def solution(mesh):
    placed = (
        P("occ", "aux", None, None),
        P("occ", "aux"),
        P("occ", "aux"),
        P("occ", None),
        P(),
        P(),
    )
    return jax.shard_map(
        per_device,
        mesh=mesh,
        in_specs=placed,
        out_specs=(P("occ", "aux", None, None), P("aux", None)),
        check_vma=False,
    )
```

profile of v0, /device:TPU:0, one launch (start us, length us, event | category | flops | bytes accessed | tf_op | source)
XLA Modules:
  0.0 811.6 jit_solution(979739568386542824)
XLA Ops:
  8.0 13.5 %all_to_all.36 = s32[8,1,1]{2,1,0:T(1,128)S(1)} all-to-all(s32[8,1,1]{2,1,0:T(1,128)S(1)} %copy.47), channel_id=1, replica_groups=mesh['occ'=8,'aux'=4] {'occ'}, dimensions={0} | all-to-all | bytes 64 | tf_op jit(solution)/shard_map/all_to_all | solution.py:37
  23.8 3.3 all-to-all-start.2
  27.1 6.7 gather_fusion.2
  33.8 6.2 all-to-all-start.3
  41.2 180.3 %all-to-all-done.3 = bf16[8,1,16,128,256]{4,3,2,1,0:T(8,128)(2,1)} async-done(((bf16[8,1,16,128,256]{4,3,2,1,0:T(8,128)(2,1)}), bf16[8,1,16,128,256]{4,3,2,1,0:T(8,128)(2,1)}, u32[]{:S(2)}, u32[]{:S(2)}) %all-to-all-start.3) | async-done | bytes 8388640 | tf_op jit(solution)/shard_map/all_to_all | solution.py:41
  221.5 3.6 all-to-all-start.1
  225.4 11.8 %copy.53 = bf16[8,16,128,256]{3,1,2,0:T(8,128)(2,1)} copy(bf16[8,16,128,256]{3,2,1,0:T(8,128)(2,1)} %bitcast.11) | data formatting | bytes 16777216
  237.2 96.8 %while.26 = (s32[]{:T(128)}, f32[8,256,256]{2,1,0:T(8,128)}, s32[8]{0:T(128)S(1)}, s32[8]{0:T(128)S(1)}, bf16[4,16,128,256]{3,2,1,0:T(8,128)(2,1)}, /*index=5*/s...) while((s32[]{:T(128)}, f32[8,256,256]{2,1,0:T(8,128)}, ...), condition=%wide.region_1.2_spmd.clone.clone, body=%wide.region_0.1_spmd.clone.clone.sunk | while | flops 285737760 | bytes 8651985 | solution.py:97
  244.8 1.7 convolution_convert_fusion.10
  256.9 1.7 convolution_convert_fusion.10
  269.0 1.7 convolution_convert_fusion.10
  281.1 1.7 convolution_convert_fusion.10
  283.2 1.3 constant_dynamic-slice_fusion.8
  293.2 1.7 convolution_convert_fusion.10
  305.3 1.7 convolution_convert_fusion.10
  317.4 1.7 convolution_convert_fusion.10
  329.5 1.7 convolution_convert_fusion.10
  335.5 51.5 %all-reduce.2.cloned.1.call-done = f32[8,256,256]{2,1,0:T(8,128)} async-done(((f32[8,256,256]{2,1,0:T(8,128)}), f32[8,256,256]{2,1,0:T(8,128)}) %all-reduce.2.cloned.1.call-update) | async-done | bytes 2097168 | tf_op jit(solution)/shard_map/psum | solution.py:98
  387.0 1.9 subtract_divide_fusion
  389.0 1.8 copy.52
  390.8 2.7 fusion.49
  393.5 115.9 %while.27 = (s32[]{:T(128)}, bf16[8,16,128,256]{3,2,1,0:T(8,128)(2,1)}, bf16[8,16,128,256]{3,2,1,0:T(8,128)(2,1)}, s32[8]{0:T(128)S(1)}, s32[8]{0:T(128)S(1)}, /...) while((s32[]{:T(128)}, ...), condition=%wide.region_4.5_spmd.clone.clone, body=%wide.region_3.4_spmd.clone.clone.sunk | while | flops 572524032 | bytes 19137928 | solution.py:133
  403.9 1.8 convolution_convert_fusion.13
  406.5 1.5 constant_dynamic-update-slice_fusion.3
  418.4 1.8 convolution_convert_fusion.13
  421.0 1.5 constant_dynamic-update-slice_fusion.3
  432.9 1.8 convolution_convert_fusion.13
  435.5 1.5 constant_dynamic-update-slice_fusion.3
  447.4 1.8 convolution_convert_fusion.13
  450.0 1.5 constant_dynamic-update-slice_fusion.3
  461.8 1.8 convolution_convert_fusion.13
  464.4 1.5 constant_dynamic-update-slice_fusion.3
  476.3 1.8 convolution_convert_fusion.13
  478.9 1.4 constant_dynamic-update-slice_fusion.3
  490.8 1.8 convolution_convert_fusion.13
  493.3 1.5 constant_dynamic-update-slice_fusion.3
  505.3 1.8 convolution_convert_fusion.13
  507.9 1.4 constant_dynamic-update-slice_fusion.3
  509.3 5.5 all-to-all-start.4
  514.9 11.6 %convert_element_type.39 = f32[8,16,128,256]{3,2,1,0:T(8,128)} convert(bf16[8,16,128,256]{3,2,1,0:T(8,128)(2,1)} %get-tuple-element.134) | non-fusion elementwise | flops 4194304 | bytes 25165824 | tf_op jit(solution)/shard_map/convert_element_type | solution.py:139
  526.5 1.3 convolution_bitcast_fusion.2
  527.8 2.5 fusion.40
  530.3 190.8 %psum.15 = bf16[64,256]{1,0:T(8,128)(2,1)S(1)} all-reduce(bf16[64,256]{1,0:T(8,128)(2,1)S(1)} %fusion.40), channel_id=1, replica_groups=mesh['occ'=8,'aux'=4] {'occ'}, use_global_device_ids=true, to_apply=%region_7.8 | all-reduce | flops 16384 | bytes 65536 | tf_op jit(solution)/shard_map/psum | solution.py:106
  721.7 4.3 broadcast_in_dim.16
  726.0 30.6 %scatter_fusion = f32[4,16,128,256]{3,2,1,0:T(8,128)} fusion(f32[4,16,128,256]{3,2,1,0:T(8,128)} %broadcast_in_dim.16, s32[8]{0:T(128)S(1)} %get-tuple-element.370, f32[8,16,128,256]{3,2,1,0:T(8,128)} %convert_element_type.39), kind=kCustom, calls=%fused_computation.5 | custom fusion | flops 4194304 | bytes 50331680 | tf_op jit(solution)/shard_map/scatter-add | solution.py:139
  756.6 11.5 %bitcast_convert_fusion = f32[8,16,128,256]{3,2,1,0:T(8,128)} fusion(bf16[8,1,16,128,256]{4,3,2,1,0:T(8,128)(2,1)} %all-to-all-done.4), kind=kLoop, calls=%fused_computation.64 | loop fusion | flops 4194304 | bytes 25165824 | tf_op jit(solution)/shard_map/convert_element_type | solution.py:140
  768.1 30.7 %scatter_fusion.1 = f32[4,16,128,256]{3,2,1,0:T(8,128)} fusion(f32[4,16,128,256]{3,2,1,0:T(8,128)} %scatter_fusion, s32[8]{0:T(128)S(1)} %fusion.44, f32[8,16,128,256]{3,2,1,0:T(8,128)} %bitcast_convert_fusion), kind=kCustom, calls=%fused_computation.6 | custom fusion | flops 4194304 | bytes 50331680 | tf_op jit(solution)/shard_map/scatter-add | solution.py:140
  798.7 6.0 convert_element_type.42
  (220 shorter events, 115.7 us)
Async XLA Ops:
  7.2 327.0 %copy-start = (f32[32]{0:T(128)S(1)}, f32[32]{0:T(128)}, u32[]{:S(2)}) copy-start(f32[32]{0:T(128)} %param.14) | copy-start | bytes 388
  23.8 10.1 %all-to-all-start.2 = ((s32[8,1,1]{2,1,0:T(1,128)}), s32[8,1,1]{2,1,0:T(1,128)S(1)}, u32[]{:S(2)}, u32[]{:S(2)}) async-start(s32[8,1,1]{2,1,0:T(1,128)} %copy.49), calls=%async_computation.2 | async-start | bytes 8192 | tf_op jit(solution)/shard_map/all_to_all | solution.py:55
  33.8 6.2 copy-start.4
  33.8 187.7 %all-to-all-start.3 = ((bf16[8,1,16,128,256]{4,3,2,1,0:T(8,128)(2,1)}), bf16[8,1,16,128,256]{4,3,2,1,0:T(8,128)(2,1)}, u32[]{:S(2)}, u32[]{:S(2)}) async-start(bf16[8,1,16,128,256]{4,3,2,1,0:T(8,128)(2,1)} %bitcast.165), calls=%async_computation.3 | async-start | bytes 16777216 | tf_op jit(solution)/shard_map/all_to_all | solution.py:41
  221.5 15.7 %all-to-all-start.1 = ((s32[8,1,16]{2,1,0:T(1,128)}), s32[8,1,16]{2,1,0:T(1,128)S(1)}, u32[]{:S(2)}, u32[]{:S(2)}) async-start(s32[8,1,16]{2,1,0:T(1,128)} %bitcast.5), calls=%async_computation.1 | async-start | bytes 8192 | tf_op jit(solution)/shard_map/all_to_all | solution.py:48
  225.1 161.9 %all-reduce.2.cloned.1.call-start = ((), (), s32[]{:S(2)}) async-start(), calls=%async_computation.5 | async-start | bytes 4194304 | tf_op jit(solution)/shard_map/psum | solution.py:98
  225.4 11.8 %copy-start.2 = (s32[4,1]{0,1:T(1,128)S(1)}, s32[4,1]{0,1:T(1,128)}, u32[]{:S(2)}) copy-start(s32[4,1]{0,1:T(1,128)} %param.12) | copy-start | bytes 52
  237.2 98.2 %copy-start.5 = (f32[256]{0:T(256)S(1)}, f32[256]{0:T(256)}, u32[]{:S(2)}) copy-start(f32[256]{0:T(256)} %param.15) | copy-start | bytes 3076
  509.3 247.3 %all-to-all-start.4 = ((bf16[8,1,16,128,256]{4,3,2,1,0:T(8,128)(2,1)}), bf16[8,1,16,128,256]{4,3,2,1,0:T(8,128)(2,1)}, u32[]{:S(2)}, u32[]{:S(2)}) async-start(bf16[8,1,16,128,256]{4,3,2,1,0:T(8,128)(2,1)} %bitcast.166), calls=%async_computation.4 | async-start | bytes 16777216 | tf_op jit(solution)/shard_map/all_to_all | solution.py:135
  514.8 11.6 %copy-start.3 = (f32[8,256,256]{1,2,0:T(8,128)S(1)}, f32[8,256,256]{1,2,0:T(8,128)}, u32[]{:S(2)}) copy-start(f32[8,256,256]{1,2,0:T(8,128)} %copy.52) | copy-start | bytes 6291460
  768.1 36.7 %copy-start.1 = (f32[32]{0:T(128)S(1)}, f32[32]{0:T(128)}, u32[]{:S(2)}) copy-start(f32[32]{0:T(128)} %param.14) | copy-start | bytes 388
Sparse Core Ops, SparseCore 0:
  334.2 52.7 all-reduce.1
where the time goes:
time: 815 us; the launch traced here: 812 us
  waiting for transfers between devices  232 us (28%)
  blocking collectives  204 us (25%)
  other arithmetic  117 us (14%)
  local copies, waits for them, and re-layouts  109 us (13%)
  loops' own time  62.4 us (8%)
  matrix products  54.3 us (7%)
  starting transfers between devices  18.7 us (2%)
  between operations  14.2 us (2%)
    psum x1, blocking collectives, per_device(): density = lax.psum(density.astype(jnp.bfloat16), 'occ').astype(jnp.float32)  191 us
    all_to_all x1, waiting for transfers between devices, per_device(): lax.all_to_all(int_tiles[asked_for].reshape(block_shape), 'occ', split_ax...  180 us
    psum x1, waiting for transfers between devices, per_device(): coulomb = lax.psum(partial_terms, 'aux')  51.5 us
    another operation x1, loops' own time, per_device(): unused, partial_terms = lax.scan(coulomb_term, 0, pair_range)  31.4 us
    another operation x1, loops' own time, per_device(): unused, parts = lax.scan(gamma_term, 0, pair_range)  31 us
    scatter-add x1, other arithmetic, per_device(): gamma_sum = gamma_sum.at[asked_for].add(returned.astype(jnp.float32))  30.7 us
    scatter-add x1, other arithmetic, per_device(): gamma_sum = gamma_sum.at[here_index].add(here_parts.astype(jnp.float32))  30.6 us
    dot_general x16, matrix products, rows_of_there(): jnp.einsum('st,tpb->spb', intersection, there_tiles[pair_index], preferre...  27.9 us
  transfers between devices with their start and end apart: 5, of which 2 were waited for; matrix products, arithmetic and copies ran while one was open for 9% of the time, Pallas kernels for 0%

commit v1 on v0

v1 whole, which is shorter than its diff:
```python
import jax
import jax.numpy as jnp
from jax import lax
from jax.experimental import pallas as pl
from jax.experimental.pallas import tpu as pltpu
from jax.sharding import PartitionSpec as P

CHUNK_TILES = 4


def slot_match(wanted_ids, source_ids):
    same = (wanted_ids[:, :, None] == source_ids[:, None, :]) & (wanted_ids[:, :, None] >= 0)
    slots = jnp.arange(source_ids.shape[1], dtype=jnp.int32)
    return jnp.max(jnp.where(same, slots[None, None, :], -1), axis=2).astype(jnp.int32)


def gather_tiles(match_ref, row, source_ref, rows_ref):
    slot_count = source_ref.shape[1]
    for slot in range(slot_count):
        found = match_ref[row, slot]

        @pl.when(found >= 0)
        def _():
            rows_ref[slot] = source_ref[0, found]

        @pl.when(found < 0)
        def _():
            rows_ref[slot] = jnp.zeros(rows_ref.shape[1:], rows_ref.dtype)


def coulomb_kernel(orb_ref, match_ref, left_ref, right_ref, out_ref, rows_ref, total_ref):
    pair = pl.program_id(0)
    slot_count, tile_rows, width = rows_ref.shape
    gather_tiles(match_ref, pair, right_ref, rows_ref)
    total_ref[...] = jnp.zeros_like(total_ref)
    chunk = min(CHUNK_TILES, slot_count)

    @pl.loop(0, slot_count // chunk)
    def _(step):
        first = step * chunk
        left = left_ref[0, pl.ds(first, chunk)].reshape(chunk * tile_rows, width)
        right = rows_ref[pl.ds(first, chunk)].reshape(chunk * tile_rows, width)
        total_ref[...] += lax.dot_general(
            left, right, (((0,), (0,)), ((), ())), preferred_element_type=jnp.float32
        )

    out_ref[0] = total_ref[...].astype(out_ref.dtype)


def coulomb_call(orbitals, match, left, own):
    pair_count, slot_count, tile_rows, width = left.shape
    block = (1, slot_count, tile_rows, width)
    return pl.pallas_call(
        coulomb_kernel,
        grid_spec=pltpu.PrefetchScalarGridSpec(
            num_scalar_prefetch=2,
            grid=(pair_count,),
            in_specs=[
                pl.BlockSpec(block, lambda p, orb, m: (p, 0, 0, 0)),
                pl.BlockSpec(block, lambda p, orb, m: (orb[p], 0, 0, 0)),
            ],
            out_specs=pl.BlockSpec((1, width, width), lambda p, orb, m: (p, 0, 0)),
            scratch_shapes=[
                pltpu.VMEM((slot_count, tile_rows, width), left.dtype),
                pltpu.VMEM((width, width), jnp.float32),
            ],
        ),
        out_shape=jax.ShapeDtypeStruct((pair_count, width, width), jnp.bfloat16),
        compiler_params=pltpu.CompilerParams(vmem_limit_bytes=32 << 20),
        cost_estimate=pl.CostEstimate(
            flops=2 * pair_count * slot_count * tile_rows * width * width,
            bytes_accessed=4 * pair_count * slot_count * tile_rows * width,
            transcendentals=0,
        ),
    )(orbitals, match, left, own)


def add_terms(transposed, orb_ref, match_ref, source_ref, weight_ref, total_ref, rows_ref):
    term = pl.program_id(0)
    slot_count, tile_rows, width = rows_ref.shape
    gather_tiles(match_ref, term, source_ref, rows_ref)
    chunk = min(CHUNK_TILES, slot_count)
    orb = orb_ref[term]

    @pl.loop(0, slot_count // chunk)
    def _(step):
        first = step * chunk
        rows = rows_ref[pl.ds(first, chunk)].reshape(chunk * tile_rows, width)
        product = lax.dot_general(
            rows,
            weight_ref[0],
            (((1,), (1 if transposed else 0,)), ((), ())),
            preferred_element_type=jnp.float32,
        )
        total_ref[orb, pl.ds(first, chunk)] += product.reshape(chunk, tile_rows, width)


def first_gamma_kernel(orb_ref, match_ref, source_ref, weight_ref, total_ref, rows_ref):
    @pl.when(pl.program_id(0) == 0)
    def _():
        total_ref[...] = jnp.zeros_like(total_ref)

    add_terms(False, orb_ref, match_ref, source_ref, weight_ref, total_ref, rows_ref)


def last_gamma_kernel(
    orb_ref, match_ref, source_ref, weight_ref, start_ref, out_ref, rows_ref, total_ref
):
    @pl.when(pl.program_id(0) == 0)
    def _():
        total_ref[...] = start_ref[...]

    add_terms(True, orb_ref, match_ref, source_ref, weight_ref, total_ref, rows_ref)

    @pl.when(pl.program_id(0) == pl.num_programs(0) - 1)
    def _():
        out_ref[...] = total_ref[...].astype(out_ref.dtype)


def gamma_call(orbitals, match, source, weights, start, orb_count):
    term_count, slot_count, tile_rows, width = source.shape
    total_shape = (orb_count, slot_count, tile_rows, width)
    whole = pl.BlockSpec(
        total_shape, lambda t, orb, m: (0, 0, 0, 0), pipeline_mode=pl.Buffered(1)
    )
    in_specs = [
        pl.BlockSpec((1, slot_count, tile_rows, width), lambda t, orb, m: (t, 0, 0, 0)),
        pl.BlockSpec((1, width, width), lambda t, orb, m: (t, 0, 0)),
    ]
    scratch = [pltpu.VMEM((slot_count, tile_rows, width), source.dtype)]
    operands = [orbitals, match, source, weights]
    if start is None:
        body, out_type = first_gamma_kernel, jnp.float32
    else:
        body, out_type = last_gamma_kernel, jnp.bfloat16
        in_specs.append(whole)
        scratch.append(pltpu.VMEM(total_shape, jnp.float32))
        operands.append(start)
    return pl.pallas_call(
        body,
        grid_spec=pltpu.PrefetchScalarGridSpec(
            num_scalar_prefetch=2,
            grid=(term_count,),
            in_specs=in_specs,
            out_specs=whole,
            scratch_shapes=scratch,
        ),
        out_shape=jax.ShapeDtypeStruct(total_shape, out_type),
        compiler_params=pltpu.CompilerParams(vmem_limit_bytes=48 << 20),
        cost_estimate=pl.CostEstimate(
            flops=2 * term_count * slot_count * tile_rows * width * width,
            bytes_accessed=2 * term_count * slot_count * tile_rows * width
            + 8 * orb_count * slot_count * tile_rows * width,
            transcendentals=0,
        ),
    )(*operands)


def exchange(blocks, axis):
    return lax.all_to_all(blocks, axis, split_axis=0, concat_axis=0, tiled=True)


def per_device(int_tiles, tile_ids, tile_counts, pair_list, occ_energy, vir_energy):
    peer_count = lax.axis_size("occ")
    group_count = lax.axis_size("aux")
    orb_count, slot_count, tile_rows, width = int_tiles.shape
    pair_count = pair_list.shape[0]
    per_peer = pair_count // peer_count
    me = lax.axis_index("occ")
    share = lax.axis_index("aux")

    here_index = pair_list[:, 0]
    left = exchange(int_tiles[here_index], "occ")

    slot_range = jnp.arange(slot_count, dtype=jnp.int32)
    live_ids = jnp.where(slot_range[None, :] < tile_counts, tile_ids, -1)
    packed = jnp.concatenate([pair_list.reshape(-1), live_ids.reshape(-1)])
    everyone = lax.all_gather(packed, "occ")
    all_pairs = everyone[:, : 2 * pair_count].reshape(peer_count, peer_count, per_peer, 2)
    all_ids = everyone[:, 2 * pair_count :].reshape(peer_count * orb_count, slot_count)
    asked = lax.dynamic_index_in_dim(all_pairs, me, 1, keepdims=False).reshape(pair_count, 2)
    source = jnp.arange(pair_count, dtype=jnp.int32) // per_peer
    left_global = source * orb_count + asked[:, 0]
    asked_for = asked[:, 1]
    left_ids = all_ids[left_global]
    right_ids = all_ids[source * orb_count + pair_list[:, 1]]
    asked_ids = live_ids[asked_for]
    coulomb_match = slot_match(left_ids, asked_ids)
    asked_match = slot_match(asked_ids, left_ids)
    here_match = slot_match(live_ids[here_index], right_ids)

    left, to_askers = lax.optimization_barrier((left, int_tiles[asked_for]))
    right = exchange(to_askers, "occ")

    partial = coulomb_call(asked_for, coulomb_match, left, int_tiles)
    share_pairs = pair_count // group_count
    parts = exchange(partial, "aux").reshape(group_count, share_pairs, width, width)
    coulomb = jnp.sum(parts.astype(jnp.float32), axis=0)
    energy_pair = occ_energy[left_global] + occ_energy[me * orb_count + asked_for]
    energy_pair = lax.dynamic_slice_in_dim(energy_pair, share * share_pairs, share_pairs, 0)
    denominator = energy_pair[:, None, None] - vir_energy[None, :, None] - vir_energy[None, None, :]
    amplitude = coulomb / denominator
    mixed = 2.0 * amplitude - jnp.swapaxes(amplitude, 1, 2)
    share_weights = mixed.astype(jnp.bfloat16)

    weights = lax.all_gather(share_weights, "aux", axis=0, tiled=True)
    row_block = width // group_count
    weight_rows = lax.dynamic_slice_in_dim(weights, share * row_block, row_block, 1)
    here_weights = lax.all_gather(exchange(weight_rows, "occ"), "aux", axis=1, tiled=True)

    density = jnp.einsum(
        "rac,rbc->ab", amplitude, mixed, precision=lax.Precision.HIGHEST
    ) + jnp.einsum("rca,rcb->ab", amplitude, mixed, precision=lax.Precision.HIGHEST)
    density = exchange(density.astype(jnp.bfloat16), "aux").reshape(group_count, row_block, width)
    density = jnp.sum(density.astype(jnp.float32), axis=0).astype(jnp.bfloat16)
    density = jnp.sum(lax.all_gather(density, "occ").astype(jnp.float32), axis=0)

    start = gamma_call(asked_for, asked_match, left, weights, None, orb_count)
    gamma = gamma_call(here_index, here_match, right, here_weights, start, orb_count)
    return gamma, density


def solution(mesh):
    placed = (
        P("occ", "aux", None, None),
        P("occ", "aux"),
        P("occ", "aux"),
        P("occ", None),
        P(),
        P(),
    )
    return jax.shard_map(
        per_device,
        mesh=mesh,
        in_specs=placed,
        out_specs=(P("occ", "aux", None, None), P("aux", None)),
        check_vma=False,
    )
```

time: 815 us -> 531 us (0.65)
  waiting for transfers between devices: 232 us -> 23.9 us
  blocking collectives: 204 us -> 396 us
  other arithmetic: 117 us -> 2.95 us
  local copies, waits for them, and re-layouts: 109 us -> 23.8 us
  loops' own time: 62.4 us -> 0 us
  matrix products: 54.3 us -> 2.73 us
  Pallas kernels: 0 us -> 46.3 us
    all_gather x0 -> x1, blocking collectives: none -> 200 us  [per_device(): lax.all_gather(density, 'occ').astype(jnp.float32)]
    psum x1 -> x0, blocking collectives: 191 us -> none  [per_device(): density = lax.psum(density.astype(jnp.bfloat16), 'occ').astype(jnp.float32)]
    unnamed x0 -> x1, blocking collectives: none -> 182 us
    all_to_all x4, waiting for transfers between devices: 180 us -> 12.9 us  [exchange(): return lax.all_to_all(blocks, axis, split_axis=0, concat_axis=0, tiled=True)]
    another operation x2 -> x0, loops' own time: 62.4 us -> none  [the longest x1 31.4 us: per_device(): unused, partial_terms = lax.scan(coulomb_term, 0, pair_range)]
    scatter-add x2 -> x0, other arithmetic: 61.3 us -> none  [the longest x1 30.7 us: per_device(): gamma_sum = gamma_sum.at[asked_for].add(returned.astype(jnp.float32))]
    dynamic_slice x80 -> x2, local copies, waits for them, and re-layouts: 59.2 us -> 1.05 us  [the longest x1 0.97 us: per_device(): lax.dynamic_slice_in_dim(weights, share * row_block, row_block, 1)]
    dot_general x50 -> x2, matrix products: 54.3 us -> 2.73 us  [the longest x1 1.9 us: per_device(): jnp.einsum('rac,rbc->ab', amplitude, mixed, precision=lax.Precision.HIGHEST)]
  transfers between devices with their start and end apart: 5 -> 6, of which waited for: 2 -> 2; matrix products, arithmetic and copies ran while one was open for 9% -> 3% of each run, Pallas kernels for 0% -> 3%
where the time goes in v1:
time: 531 us; the launch traced here: 530 us
  blocking collectives  396 us (75%)
  Pallas kernels  46.3 us (9%)
  waiting for transfers between devices  23.9 us (5%)
  local copies, waits for them, and re-layouts  23.8 us (4%)
  starting transfers between devices  19.4 us (4%)
  between operations  14.9 us (3%)
    all_gather x1, blocking collectives, per_device(): lax.all_gather(density, 'occ').astype(jnp.float32)  200 us
    unnamed x1, blocking collectives  182 us
    pallas_call x2, Pallas kernels, gamma_call(): pl.pallas_call(body, grid_spec=pltpu.PrefetchScalarGridSpec(num_scalar_pr...  32.8 us
    all_to_all x4, starting transfers between devices, exchange(): return lax.all_to_all(blocks, axis, split_axis=0, concat_axis=0, tiled=True)  19.3 us
    all_to_all x1, blocking collectives, exchange(): return lax.all_to_all(blocks, axis, split_axis=0, concat_axis=0, tiled=True)  14.2 us
    pallas_call x1, Pallas kernels, coulomb_call(): pl.pallas_call(coulomb_kernel, grid_spec=pltpu.PrefetchScalarGridSpec(num...  13.5 us
    all_to_all x4, waiting for transfers between devices, exchange(): return lax.all_to_all(blocks, axis, split_axis=0, concat_axis=0, tiled=True)  12.9 us
  transfers between devices with their start and end apart: 6, of which 2 were waited for; matrix products, arithmetic and copies ran while one was open for 3% of the time, Pallas kernels for 3%

profile of v1, /device:TPU:0, one launch (start us, length us, event | category | flops | bytes accessed | tf_op | source)
XLA Modules:
  0.0 529.9 jit_solution(7310522841835815285)
XLA Ops:
  7.2 0.8 fusion.4
  7.9 6.8 %gather_fusion.2 = bf16[8,16,128,256]{3,2,1,0:T(8,128)(2,1)} fusion(bf16[4,16,128,256]{3,2,1,0:T(8,128)(2,1)} %right_ref.1, s32[1024]{0:T(1024)S(1)} %pad_clamp_fusion.4), kind=kCustom, calls=%fused_computation.2 | custom fusion | bytes 16777248 | tf_op jit(solution)/shard_map/gather | solution.py:173
  14.8 7.4 %all-to-all-start = ((bf16[8,16,128,256]{3,2,1,0:T(8,128)(2,1)}), bf16[8,16,128,256]{3,2,1,0:T(8,128)(2,1)}, u32[]{:S(2)}, u32[]{:S(2)}) async-start(bf16[8,16,128,256]{3,2,1,0:T(8,128)(2,1)} %gather_fusion.2), calls=%async_computation | async-start | bytes 16777216 | tf_op jit(solution)/shard_map/all_to_all | solution.py:160
  22.2 0.1 copy.23
  22.2 0.1 fusion.3
  22.3 0.1 reshape.87
  22.4 0.1 reshape.86
  22.5 0.6 dynamic-slice
  23.7 0.2 add_dynamic-update-slice_fusion
  23.9 181.5 %all-reduce = s32[640]{0:T(1024)S(1)} all-reduce(s32[640]{0:T(1024)S(1)} %add_dynamic-update-slice_fusion), channel_id=2, replica_groups=mesh['occ'=8,'aux'=4] {'occ'}, use_global_device_ids=true, to_apply=%add | all-reduce | flops 640 | bytes 5120
  205.5 0.1 reshape.156
  205.5 0.1 slice.19
  205.6 0.1 copy.24
  205.7 0.6 gather_fusion.5
  206.3 6.8 %gather_fusion.3 = bf16[8,16,128,256]{3,2,1,0:T(8,128)(2,1)} fusion(bf16[4,16,128,256]{3,2,1,0:T(8,128)(2,1)} %right_ref.1, s32[1024]{0:T(1024)S(1)} %pad_clamp_fusion.2), kind=kCustom, calls=%fused_computation.3 | custom fusion | bytes 16777248 | tf_op jit(solution)/shard_map/gather | solution.py:192
  213.1 0.1 reshape.88
  213.2 0.6 gather_fusion.4
  213.7 0.4 select_reduce_fusion
  214.2 2.2 copy-done.1
  216.4 13.5 %shard_map.77 = bf16[8,256,256]{2,1,0:T(8,128)(2,1)} custom-call(s32[8]{0:T(128)S(1)} %get-tuple-element.8.orb_ref, s32[8,16]{1,0:T(8,128)S(1)} %get-tuple-element.7.match_ref, bf16[8,16,128,256]{3,2,1,0:T(8,128)(2,1)} %all-to-all-done.left_ref.source_ref, bf16[4,16,128,256]{3,2,1,0:T(8,128)(2,1)S(1)} %copy-done.1), custom_call_target="tpu_custom_call" | custom-call | flops 2147483648 | bytes 16777216 | tf_op jit(solution)/shard_map/pallas_call | solution.py:53
  229.9 3.5 all-to-all-start.2
  233.4 0.0 all-gather.5.cloned.1.call-start
  233.5 0.6 gather_fusion.6
  234.1 0.6 gather_fusion.7
  234.8 0.1 dynamic_slice.11
  234.8 0.1 broadcast_subtract_fusion
  234.9 12.9 %all-to-all-done.2 = bf16[8,256,256]{2,1,0:T(8,128)(2,1)S(1)} async-done(((bf16[8,256,256]{2,1,0:T(8,128)(2,1)}), bf16[8,256,256]{2,1,0:T(8,128)(2,1)S(1)}, u32[]{:S(2)}, u32[]{:S(2)}) %all-to-all-start.2) | async-done | bytes 1048608 | tf_op jit(solution)/shard_map/all_to_all | solution.py:160
  247.8 0.1 convert_reduce_fusion
  248.0 0.2 copy.25
  248.2 0.2 fusion.11
  248.4 0.8 copy.26
  249.3 0.8 convolution_bitcast_fusion
  250.1 1.9 fusion.1
  252.0 3.3 all-to-all-start.4
  255.3 10.3 %all-gather.5.cloned.1.call-done.weight_ref = bf16[8,256,256]{2,1,0:T(8,128)(2,1)} async-done(((bf16[2,256,256]{2,1,0:T(8,128)(2,1)}), bf16[8,256,256]{2,1,0:T(8,128)(2,1)}) %all-gather.5.cloned.1.call-update) | async-done | bytes 1048592 | tf_op jit(solution)/shard_map/all_gather | solution.py:206
  265.6 1.0 constant_dynamic-slice_fusion
  266.6 14.2 %all_to_all.29 = bf16[8,64,256]{2,1,0:T(8,128)(2,1)} all-to-all(bf16[8,64,256]{2,1,0:T(8,128)(2,1)S(1)} %constant_dynamic-slice_fusion), channel_id=1, replica_groups=mesh['occ'=8,'aux'=4] {'occ'}, dimensions={0} | all-to-all | bytes 524288 | tf_op jit(solution)/shard_map/all_to_all | solution.py:160
  280.8 5.1 all-to-all-start.1
  285.9 0.0 all-gather.7.cloned.1.call-start
  286.0 0.7 all-gather.7.cloned.1.call-update
  286.7 0.6 gather_fusion
  287.2 0.6 gather_fusion.1
  287.8 0.3 select_reduce_fusion.2.match_ref
  288.1 200.2 %all-gather.1 = bf16[512,256]{1,0:T(8,128)(2,1)S(1)} all-gather(bf16[64,256]{1,0:T(8,128)(2,1)S(1)} %reduce_sum.34), channel_id=3, replica_groups=mesh['occ'=8,'aux'=4] {'occ'}, dimensions={0}, use_global_device_ids=true | all-gather | bytes 294912 | tf_op jit(solution)/shard_map/all_gather | solution.py:216
  488.3 0.7 convert_reduce_fusion.1
  489.0 15.0 %shard_map.78.start_ref = f32[4,16,128,256]{3,2,1,0:T(8,128)} custom-call(s32[8]{0:T(128)S(1)} %get-tuple-element.8.orb_ref, s32[8,16]{1,0:T(8,128)S(1)} %get-tuple-element.6.match_ref, bf16[8,16,128,256]{3,2,1,0:T(8,128)(2,1)} %all-to-all-done.left_ref.source_ref, bf16[8,256,256]{2,1,0:T(8,128)(2,1)S(1)} %copy-done.2), custom_call_target="tpu_custom_call" | custom-call | flops 2147483648 | bytes 25165824 | tf_op jit(solution)/shard_map/pallas_call | solution.py:139
  504.0 1.2 copy-done.3
  505.2 17.8 %shard_map.79 = bf16[4,16,128,256]{3,2,1,0:T(8,128)(2,1)} custom-call(s32[8]{0:T(128)S(1)} %get-tuple-element.13.orb_ref, s32[8,16]{1,0:T(8,128)S(1)} %select_reduce_fusion.2.match_ref, bf16[8,16,128,256]{3,2,1,0:T(8,128)(2,1)} %all-to-all-done.1.source_ref, bf16[8,256,256]{2,1,0:T(8,128)(2,1)S(1)} %copy-done.3, f32[4,16,128,256]{3,2,1,0:T(8,128)} %shard_map.78.start_ref), custom_call_target="tpu_custom_call" | custom-call | flops 2147483648 | bytes 25165824 | tf_op jit(solution)/shard_map/pallas_call | solution.py:139
  (33 shorter events, 0.1 us)
Async XLA Ops:
  7.2 226.3 %copy-start = (f32[32]{0:T(128)S(1)}, f32[32]{0:T(128)}, u32[]{:S(2)}) copy-start(f32[32]{0:T(128)} %param.10) | copy-start | bytes 388
  14.7 7.4 %copy-start.5 = (s32[8,2]{0,1:T(2,128)S(1)}, s32[8,2]{0,1:T(2,128)}, u32[]{:S(2)}) copy-start(s32[8,2]{0,1:T(2,128)} %param.9) | copy-start | bytes 196
  14.7 7.5 %copy-start.6 = (s32[4,16]{1,0:T(4,128)S(1)}, s32[4,16]{1,0:T(4,128)}, u32[]{:S(2)}) copy-start(s32[4,16]{1,0:T(4,128)} %param.7) | copy-start | bytes 772
  14.8 7.5 %copy-start.7 = (s32[4,1]{0,1:T(1,128)S(1)}, s32[4,1]{0,1:T(1,128)}, u32[]{:S(2)}) copy-start(s32[4,1]{0,1:T(1,128)} %param.8) | copy-start | bytes 52
  14.8 7.7 %copy-start.8 = (u32[32]{0:T(128)S(1)}, u32[32]{0:T(128)}, u32[]{:S(2)}) copy-start(u32[32]{0:T(128)} %constant.58) | copy-start | bytes 388
  14.8 199.4 %all-to-all-start = ((bf16[8,16,128,256]{3,2,1,0:T(8,128)(2,1)}), bf16[8,16,128,256]{3,2,1,0:T(8,128)(2,1)}, u32[]{:S(2)}, u32[]{:S(2)}) async-start(bf16[8,16,128,256]{3,2,1,0:T(8,128)(2,1)} %gather_fusion.2), calls=%async_computation | async-start | bytes 16777216 | tf_op jit(solution)/shard_map/all_to_all | solution.py:160
  214.2 2.2 copy-start.1
  216.4 18.5 %copy-start.4 = (f32[256]{0:T(256)S(1)}, f32[256]{0:T(256)}, u32[]{:S(2)}) copy-start(f32[256]{0:T(256)} %param.11) | copy-start | bytes 3076
  229.9 18.0 %all-to-all-start.2 = ((bf16[8,256,256]{2,1,0:T(8,128)(2,1)}), bf16[8,256,256]{2,1,0:T(8,128)(2,1)S(1)}, u32[]{:S(2)}, u32[]{:S(2)}) async-start(bf16[8,256,256]{2,1,0:T(8,128)(2,1)} %shard_map.77), calls=%async_computation.2 | async-start | bytes 2097152 | tf_op jit(solution)/shard_map/all_to_all | solution.py:160
  233.4 32.2 %all-gather.5.cloned.1.call-start = ((), (), s32[]{:S(2)}) async-start(), calls=%async_computation.5 | async-start | bytes 1310720 | tf_op jit(solution)/shard_map/all_gather | solution.py:206
  252.0 14.6 %all-to-all-start.4 = ((bf16[4,64,256]{2,1,0:T(8,128)(2,1)}), bf16[4,64,256]{2,1,0:T(8,128)(2,1)S(1)}, u32[]{:S(2)}, u32[]{:S(2)}) async-start(bf16[4,64,256]{2,1,0:T(8,128)(2,1)} %bitcast.15), calls=%async_computation.4 | async-start | bytes 262144 | tf_op jit(solution)/shard_map/all_to_all | solution.py:160
  280.8 208.1 %copy-start.2 = (bf16[8,256,256]{2,1,0:T(8,128)(2,1)S(1)}, bf16[8,256,256]{2,1,0:T(8,128)(2,1)}, u32[]{:S(2)}) copy-start(bf16[8,256,256]{2,1,0:T(8,128)(2,1)} %all-gather.5.cloned.1.call-done.weight_ref) | copy-start | bytes 3145732
  280.8 223.2 %all-to-all-start.1 = ((bf16[8,16,128,256]{3,2,1,0:T(8,128)(2,1)}), bf16[8,16,128,256]{3,2,1,0:T(8,128)(2,1)}, u32[]{:S(2)}, u32[]{:S(2)}) async-start(bf16[8,16,128,256]{3,2,1,0:T(8,128)(2,1)} %gather_fusion.3), calls=%async_computation.1 | async-start | bytes 16777216 | tf_op jit(solution)/shard_map/all_to_all | solution.py:160
  285.9 218.1 %all-gather.7.cloned.1.call-start = ((), (), s32[]{:S(2)}) async-start(), calls=%async_computation.6 | async-start | bytes 1310720 | tf_op jit(solution)/shard_map/all_gather | solution.py:209
  504.0 1.2 copy-start.3
Sparse Core Ops, SparseCore 0:
  249.4 16.1 all-gather.4
  288.3 17.0 all-gather.6

commit v2 on v1

--- a/solution.py
+++ b/solution.py
@@ -75,7 +75,7 @@
     )(orbitals, match, left, own)
 
 
-def add_terms(transposed, orb_ref, match_ref, source_ref, weight_ref, total_ref, rows_ref):
+def add_terms(orb_ref, match_ref, source_ref, weight_ref, total_ref, rows_ref):
     term = pl.program_id(0)
     slot_count, tile_rows, width = rows_ref.shape
     gather_tiles(match_ref, term, source_ref, rows_ref)
@@ -89,7 +89,7 @@
         product = lax.dot_general(
             rows,
             weight_ref[0],
-            (((1,), (1 if transposed else 0,)), ((), ())),
+            (((1,), (0,)), ((), ())),
             preferred_element_type=jnp.float32,
         )
         total_ref[orb, pl.ds(first, chunk)] += product.reshape(chunk, tile_rows, width)
@@ -100,7 +100,7 @@
     def _():
         total_ref[...] = jnp.zeros_like(total_ref)
 
-    add_terms(False, orb_ref, match_ref, source_ref, weight_ref, total_ref, rows_ref)
+    add_terms(orb_ref, match_ref, source_ref, weight_ref, total_ref, rows_ref)
 
 
 def last_gamma_kernel(
@@ -110,7 +110,7 @@
     def _():
         total_ref[...] = start_ref[...]
 
-    add_terms(True, orb_ref, match_ref, source_ref, weight_ref, total_ref, rows_ref)
+    add_terms(orb_ref, match_ref, source_ref, weight_ref, total_ref, rows_ref)
 
     @pl.when(pl.program_id(0) == pl.num_programs(0) - 1)
     def _():
@@ -157,66 +157,117 @@
 
 
 def exchange(blocks, axis):
-    return lax.all_to_all(blocks, axis, split_axis=0, concat_axis=0, tiled=True)
+    count = lax.axis_size(axis)
+    me = lax.axis_index(axis)
+    arrived = [lax.dynamic_index_in_dim(blocks, me, 0, keepdims=False)]
+    for shift in range(1, count):
+        block = lax.dynamic_index_in_dim(blocks, lax.rem(me + shift, count), 0, keepdims=False)
+        arrived.append(lax.ppermute(block, axis, [(d, (d + shift) % count) for d in range(count)]))
+    return arrived
+
+
+def sum_everywhere(block, axis):
+    count = lax.axis_size(axis)
+    total = block.astype(jnp.float32)
+    for shift in range(1, count):
+        moved = lax.ppermute(block, axis, [(d, (d + shift) % count) for d in range(count)])
+        total = total + moved.astype(jnp.float32)
+    return total
+
+
+def pair_weights(partial, energy_pair, vir_energy):
+    group_count = lax.axis_size("aux")
+    share = lax.axis_index("aux")
+    term_count, width = partial.shape[:2]
+    share_terms = term_count // group_count
+    parts = exchange(partial.reshape(group_count, share_terms, width, width), "aux")
+    coulomb = parts[0].astype(jnp.float32)
+    for part in parts[1:]:
+        coulomb = coulomb + part.astype(jnp.float32)
+    energy = lax.dynamic_slice_in_dim(energy_pair, share * share_terms, share_terms, 0)
+    denominator = energy[:, None, None] - vir_energy[None, :, None] - vir_energy[None, None, :]
+    amplitude = coulomb / denominator
+    mixed = 2.0 * amplitude - jnp.swapaxes(amplitude, 1, 2)
+    weights = lax.all_gather(mixed.astype(jnp.bfloat16), "aux", axis=0, tiled=True)
+    amplitude, mixed = amplitude[0::2], mixed[0::2]
+    density = jnp.einsum(
+        "rac,rbc->ab", amplitude, mixed, precision=lax.Precision.HIGHEST
+    ) + jnp.einsum("rca,rcb->ab", amplitude, mixed, precision=lax.Precision.HIGHEST)
+    return weights, density
 
 
 def per_device(int_tiles, tile_ids, tile_counts, pair_list, occ_energy, vir_energy):
     peer_count = lax.axis_size("occ")
     group_count = lax.axis_size("aux")
     orb_count, slot_count, tile_rows, width = int_tiles.shape
-    pair_count = pair_list.shape[0]
-    per_peer = pair_count // peer_count
+    assert pair_list.shape[0] == peer_count and peer_count % 2 == 0
+    half = peer_count // 2
+    assert (2 * half) % (2 * group_count) == 0
     me = lax.axis_index("occ")
-    share = lax.axis_index("aux")
-
-    here_index = pair_list[:, 0]
-    left = exchange(int_tiles[here_index], "occ")
 
     slot_range = jnp.arange(slot_count, dtype=jnp.int32)
     live_ids = jnp.where(slot_range[None, :] < tile_counts, tile_ids, -1)
     packed = jnp.concatenate([pair_list.reshape(-1), live_ids.reshape(-1)])
     everyone = lax.all_gather(packed, "occ")
-    all_pairs = everyone[:, : 2 * pair_count].reshape(peer_count, peer_count, per_peer, 2)
-    all_ids = everyone[:, 2 * pair_count :].reshape(peer_count * orb_count, slot_count)
-    asked = lax.dynamic_index_in_dim(all_pairs, me, 1, keepdims=False).reshape(pair_count, 2)
-    source = jnp.arange(pair_count, dtype=jnp.int32) // per_peer
-    left_global = source * orb_count + asked[:, 0]
-    asked_for = asked[:, 1]
-    left_ids = all_ids[left_global]
-    right_ids = all_ids[source * orb_count + pair_list[:, 1]]
-    asked_ids = live_ids[asked_for]
-    coulomb_match = slot_match(left_ids, asked_ids)
-    asked_match = slot_match(asked_ids, left_ids)
-    here_match = slot_match(live_ids[here_index], right_ids)
-
-    left, to_askers = lax.optimization_barrier((left, int_tiles[asked_for]))
-    right = exchange(to_askers, "occ")
-
-    partial = coulomb_call(asked_for, coulomb_match, left, int_tiles)
-    share_pairs = pair_count // group_count
-    parts = exchange(partial, "aux").reshape(group_count, share_pairs, width, width)
-    coulomb = jnp.sum(parts.astype(jnp.float32), axis=0)
-    energy_pair = occ_energy[left_global] + occ_energy[me * orb_count + asked_for]
-    energy_pair = lax.dynamic_slice_in_dim(energy_pair, share * share_pairs, share_pairs, 0)
-    denominator = energy_pair[:, None, None] - vir_energy[None, :, None] - vir_energy[None, None, :]
-    amplitude = coulomb / denominator
-    mixed = 2.0 * amplitude - jnp.swapaxes(amplitude, 1, 2)
-    share_weights = mixed.astype(jnp.bfloat16)
-
-    weights = lax.all_gather(share_weights, "aux", axis=0, tiled=True)
-    row_block = width // group_count
-    weight_rows = lax.dynamic_slice_in_dim(weights, share * row_block, row_block, 1)
-    here_weights = lax.all_gather(exchange(weight_rows, "occ"), "aux", axis=1, tiled=True)
-
-    density = jnp.einsum(
-        "rac,rbc->ab", amplitude, mixed, precision=lax.Precision.HIGHEST
-    ) + jnp.einsum("rca,rcb->ab", amplitude, mixed, precision=lax.Precision.HIGHEST)
-    density = exchange(density.astype(jnp.bfloat16), "aux").reshape(group_count, row_block, width)
-    density = jnp.sum(density.astype(jnp.float32), axis=0).astype(jnp.bfloat16)
-    density = jnp.sum(lax.all_gather(density, "occ").astype(jnp.float32), axis=0)
-
-    start = gamma_call(asked_for, asked_match, left, weights, None, orb_count)
-    gamma = gamma_call(here_index, here_match, right, here_weights, start, orb_count)
+    everyone, own_tiles = lax.optimization_barrier((everyone, int_tiles))
+    all_pairs = everyone[:, : 2 * peer_count].reshape(peer_count, peer_count, 2)
+    all_ids = everyone[:, 2 * peer_count :].reshape(peer_count * orb_count, slot_count)
+
+    near = me // half * half + jnp.arange(half, dtype=jnp.int32)
+    far = lax.rem(near + half, peer_count)
+    partner = lax.rem(me + half, peer_count)
+
+    def wanted_of(owner):
+        return jnp.stack([all_pairs[owner, near, 0], all_pairs[near, owner, 1]], axis=1).reshape(-1)
+
+    def terms_of(peers):
+        remote = jnp.stack([all_pairs[peers, me, 0], all_pairs[me, peers, 1]], axis=1)
+        own = jnp.stack([all_pairs[peers, me, 1], all_pairs[me, peers, 0]], axis=1).reshape(-1)
+        remote = (peers[:, None] * orb_count + remote).reshape(-1)
+        remote_ids, own_ids = all_ids[remote], live_ids[own]
+        energy_pair = occ_energy[remote] + occ_energy[me * orb_count + own]
+        return (
+            own,
+            slot_match(remote_ids, own_ids),
+            slot_match(own_ids, remote_ids),
+            energy_pair,
+        )
+
+    groups = [list(range(half)), list(range(half, peer_count))]
+
+    def near_exchange(tiles, owner):
+        return lax.all_to_all(
+            tiles[wanted_of(owner)],
+            "occ",
+            split_axis=0,
+            concat_axis=0,
+            axis_index_groups=groups,
+            tiled=True,
+        )
+
+    swapped = [(d, (d + half) % peer_count) for d in range(peer_count)]
+    partner_tiles = lax.ppermute(own_tiles, "occ", swapped)
+    near_tiles = near_exchange(own_tiles, me)
+    far_tiles = near_exchange(partner_tiles, partner)
+
+    own, coulomb_match, near_match, energy_pair = terms_of(near)
+    partial = coulomb_call(own, coulomb_match, near_tiles, int_tiles)
+    weights, density = pair_weights(partial, energy_pair, vir_energy)
+    gamma = gamma_call(own, near_match, near_tiles, weights, None, orb_count)
+
+    far_tiles, gamma = lax.optimization_barrier((far_tiles, gamma))
+    own, coulomb_match, far_match, energy_pair = terms_of(far)
+    partial = coulomb_call(own, coulomb_match, far_tiles, int_tiles)
+    weights, more_density = pair_weights(partial, energy_pair, vir_energy)
+
+    density = (density + more_density).astype(jnp.bfloat16)
+    parts = exchange(density.reshape(group_count, width // group_count, width), "aux")
+    density = parts[0].astype(jnp.float32)
+    for part in parts[1:]:
+        density = density + part.astype(jnp.float32)
+    density = sum_everywhere(density.astype(jnp.bfloat16), "occ")
+
+    gamma = gamma_call(own, far_match, far_tiles, weights, gamma, orb_count)
     return gamma, density
 
 

time: 531 us -> 396 us (0.75)
  blocking collectives: 396 us -> 13.1 us
  waiting for transfers between devices: 23.9 us -> 232 us
  local copies, waits for them, and re-layouts: 23.8 us -> 37.7 us
  starting transfers between devices: 19.4 us -> 32.9 us
  Pallas kernels: 46.3 us -> 57.5 us
    ppermute x0 -> x17, waiting for transfers between devices: none -> 203 us  [the longest x1 179 us: per_device(): partner_tiles = lax.ppermute(own_tiles, 'occ', swapped)]
    all_gather x1 -> x0, blocking collectives: 200 us -> none  [per_device(): lax.all_gather(density, 'occ').astype(jnp.float32)]
    unnamed x1, blocking collectives: 182 us -> 13.1 us
    ppermute x0 -> x17, starting transfers between devices: none -> 21.5 us  [the longest x7 12.5 us: sum_everywhere(): lax.ppermute(block, axis, [(d, (d + shift) % count) for d in range(count)])]
    all_to_all x1 -> x0, blocking collectives: 14.2 us -> none  [exchange(): return lax.all_to_all(blocks, axis, split_axis=0, concat_axis=0, tiled=True)]
    pallas_call x1 -> x2, Pallas kernels: 13.5 us -> 25.6 us  [coulomb_call(): pl.pallas_call(coulomb_kernel, grid_spec=pltpu.PrefetchScalarGridSpec(num...]
    all_to_all x4 -> x2, starting transfers between devices: 19.3 us -> 11.3 us  [near_exchange(): lax.all_to_all(tiles[wanted_of(owner)], 'occ', split_axis=0, concat_axis=...]
    gather x8 -> x20, local copies, waits for them, and re-layouts: 17.1 us -> 24.8 us  [the longest x2 13.5 us: near_exchange(): tiles[wanted_of(owner)]]
  transfers between devices with their start and end apart: 6 -> 21, of which waited for: 2 -> 13; matrix products, arithmetic and copies ran while one was open for 3% -> 6% of each run, Pallas kernels for 3% -> 7%
where the time goes in v2:
time: 396 us; the launch traced here: 395 us
  waiting for transfers between devices  232 us (59%)
  Pallas kernels  57.5 us (15%)
  local copies, waits for them, and re-layouts  37.7 us (10%)
  starting transfers between devices  32.9 us (8%)
  between operations  15.1 us (4%)
  blocking collectives  13.1 us (3%)
  other arithmetic  4.28 us (1%)
    ppermute x1, waiting for transfers between devices, per_device(): partner_tiles = lax.ppermute(own_tiles, 'occ', swapped)  179 us
    pallas_call x2, Pallas kernels, gamma_call(): pl.pallas_call(body, grid_spec=pltpu.PrefetchScalarGridSpec(num_scalar_pr...  31.8 us
    pallas_call x2, Pallas kernels, coulomb_call(): pl.pallas_call(coulomb_kernel, grid_spec=pltpu.PrefetchScalarGridSpec(num...  25.6 us
    ppermute x9, waiting for transfers between devices, exchange(): lax.ppermute(block, axis, [(d, (d + shift) % count) for d in range(count)])  22 us
    all_gather x2, waiting for transfers between devices, pair_weights(): lax.all_gather(mixed.astype(jnp.bfloat16), 'aux', axis=0, tiled=True)  16.7 us
    gather x2, local copies, waits for them, and re-layouts, near_exchange(): tiles[wanted_of(owner)]  13.5 us
    unnamed x1, blocking collectives  13.1 us
    all_to_all x2, waiting for transfers between devices, near_exchange(): lax.all_to_all(tiles[wanted_of(owner)], 'occ', split_axis=0, concat_axis=...  12.7 us
  transfers between devices with their start and end apart: 21, of which 13 were waited for; matrix products, arithmetic and copies ran while one was open for 6% of the time, Pallas kernels for 7%

profile of v2, /device:TPU:0, one launch (start us, length us, event | category | flops | bytes accessed | tf_op | source)
XLA Modules:
  0.0 394.9 jit_solution(18364138298869967986)
XLA Ops:
  7.2 0.8 fusion.13
  8.0 0.8 copy.56
  8.9 1.2 dynamic-slice
  11.0 13.1 %all-reduce = s32[640]{0:T(1024)S(1)} all-reduce(s32[640]{0:T(1024)S(1)} %add_dynamic-update-slice_fusion), channel_id=2, replica_groups=mesh['occ'=8,'aux'=4] {'occ'}, use_global_device_ids=true, to_apply=%add | all-reduce | flops 640 | bytes 5120
  24.9 0.7 gather_fusion.10
  25.7 6.7 %gather_fusion.15 = bf16[8,16,128,256]{3,2,1,0:T(8,128)(2,1)} fusion(bf16[4,16,128,256]{3,2,1,0:T(8,128)(2,1)} %right_ref.3, s32[1024]{0:T(1024)S(1)} %pad_clamp_fusion.2), kind=kCustom, calls=%fused_computation.15 | custom fusion | bytes 16777248 | tf_op jit(solution)/shard_map/gather | solution.py:240
  32.5 5.7 %all-to-all-start.1 = ((bf16[8,16,128,256]{3,2,1,0:T(8,128)(2,1)}), bf16[8,16,128,256]{3,2,1,0:T(8,128)(2,1)}, u32[]{:S(2)}, u32[]{:S(2)}) async-start(bf16[8,16,128,256]{3,2,1,0:T(8,128)(2,1)} %gather_fusion.15), calls=%async_computation.1 | async-start | bytes 16777216 | tf_op jit(solution)/shard_map/all_to_all | solution.py:239
  39.3 0.7 gather_fusion.7
  40.1 178.6 %collective-permute-done = bf16[4,16,128,256]{3,2,1,0:T(8,128)(2,1)} collective-permute-done((bf16[4,16,128,256]{3,2,1,0:T(8,128)(2,1)}, bf16[4,16,128,256]{3,2,1,0:T(8,128)(2,1)}, u32[]{:S(2)}, u32[]{:S(2)}) %collective-permute-start) | collective-permute-done | bytes 4194336 | tf_op jit(solution)/shard_map/ppermute | solution.py:249
  218.8 6.8 %gather_fusion.8 = bf16[8,16,128,256]{3,2,1,0:T(8,128)(2,1)} fusion(bf16[4,16,128,256]{3,2,1,0:T(8,128)(2,1)} %collective-permute-done, s32[1024]{0:T(1024)S(1)} %pad_clamp_fusion.5), kind=kCustom, calls=%fused_computation.8 | custom fusion | bytes 16777248 | tf_op jit(solution)/shard_map/gather | solution.py:240
  225.5 5.7 %all-to-all-start = ((bf16[8,16,128,256]{3,2,1,0:T(8,128)(2,1)}), bf16[8,16,128,256]{3,2,1,0:T(8,128)(2,1)}, u32[]{:S(2)}, u32[]{:S(2)}) async-start(bf16[8,16,128,256]{3,2,1,0:T(8,128)(2,1)} %gather_fusion.8), calls=%async_computation | async-start | bytes 16777216 | tf_op jit(solution)/shard_map/all_to_all | solution.py:239
  231.6 0.7 gather_fusion.12
  233.9 0.7 gather_fusion.4
  237.8 0.7 gather_fusion
  238.5 0.7 gather_fusion.1
  241.8 2.2 copy-done.2
  244.0 12.8 %shard_map.77 = bf16[8,256,256]{2,1,0:T(8,128)(2,1)S(1)} custom-call(s32[8]{0:T(128)S(1)} %reshape.420.orb_ref, s32[8,16]{1,0:T(8,128)S(1)} %get-tuple-element.12.match_ref, bf16[8,16,128,256]{3,2,1,0:T(8,128)(2,1)} %all-to-all-done.1.left_ref.source_ref, bf16[4,16,128,256]{3,2,1,0:T(8,128)(2,1)S(1)} %copy-done.2), custom_call_target="tpu_custom_call" | custom-call | flops 2147483648 | bytes 16777216 | tf_op jit(solution)/shard_map/pallas_call | solution.py:53
  257.3 1.6 collective-permute-start.2
  259.0 1.5 collective-permute-start.3
  261.1 3.9 collective-permute-done.1
  265.0 1.5 collective-permute-done.2
  266.5 3.9 collective-permute-done.3
  270.8 0.8 fusion.31
  272.2 16.7 %all-gather.4.cloned.1.call-done.weight_ref = bf16[8,256,256]{2,1,0:T(8,128)(2,1)} async-done(((bf16[2,256,256]{2,1,0:T(8,128)(2,1)}), bf16[8,256,256]{2,1,0:T(8,128)(2,1)}) %all-gather.4.cloned.1.call-update) | async-done | bytes 1048592 | tf_op jit(solution)/shard_map/all_gather | solution.py:191
  288.9 1.2 copy-done.4
  290.1 15.1 %shard_map.78.start_ref = f32[4,16,128,256]{3,2,1,0:T(8,128)} custom-call(s32[8]{0:T(128)S(1)} %reshape.420.orb_ref, s32[8,16]{1,0:T(8,128)S(1)} %get-tuple-element.13.match_ref, bf16[8,16,128,256]{3,2,1,0:T(8,128)(2,1)} %all-to-all-done.1.left_ref.source_ref, bf16[8,256,256]{2,1,0:T(8,128)(2,1)S(1)} %copy-done.4), custom_call_target="tpu_custom_call" | custom-call | flops 2147483648 | bytes 25165824 | tf_op jit(solution)/shard_map/pallas_call | solution.py:139
  305.2 12.7 %all-to-all-done.left_ref.source_ref = bf16[8,16,128,256]{3,2,1,0:T(8,128)(2,1)} async-done(((bf16[8,16,128,256]{3,2,1,0:T(8,128)(2,1)}), bf16[8,16,128,256]{3,2,1,0:T(8,128)(2,1)}, u32[]{:S(2)}, u32[]{:S(2)}) %all-to-all-start) | async-done | bytes 8388640 | tf_op jit(solution)/shard_map/all_to_all | solution.py:239
  317.9 2.2 copy-done.3
  320.1 12.8 %shard_map.79 = bf16[8,256,256]{2,1,0:T(8,128)(2,1)S(1)} custom-call(s32[8]{0:T(128)S(1)} %reshape.416.orb_ref, s32[8,16]{1,0:T(8,128)S(1)} %get-tuple-element.10.match_ref, bf16[8,16,128,256]{3,2,1,0:T(8,128)(2,1)} %all-to-all-done.left_ref.source_ref, bf16[4,16,128,256]{3,2,1,0:T(8,128)(2,1)S(1)} %copy-done.3), custom_call_target="tpu_custom_call" | custom-call | flops 2147483648 | bytes 16777216 | tf_op jit(solution)/shard_map/pallas_call | solution.py:53
  333.0 1.6 collective-permute-start.5
  334.6 1.4 collective-permute-start.6
  336.0 5.0 %collective-permute-done.4 = bf16[2,256,256]{2,1,0:T(8,128)(2,1)S(1)} collective-permute-done((bf16[2,256,256]{2,1,0:T(8,128)(2,1)S(1)}, bf16[2,256,256]{2,1,0:T(8,128)(2,1)S(1)}, u32[]{:S(2)}, u32[]{:S(2)}) %collective-permute-start.4) | collective-permute-done | bytes 262176 | tf_op jit(solution)/shard_map/ppermute | solution.py:165
  341.0 1.2 collective-permute-done.5
  342.2 4.1 %collective-permute-done.6 = bf16[2,256,256]{2,1,0:T(8,128)(2,1)S(1)} collective-permute-done((bf16[2,256,256]{2,1,0:T(8,128)(2,1)S(1)}, bf16[2,256,256]{2,1,0:T(8,128)(2,1)S(1)}, u32[]{:S(2)}, u32[]{:S(2)}) %collective-permute-start.6) | collective-permute-done | bytes 262176 | tf_op jit(solution)/shard_map/ppermute | solution.py:165
  346.7 0.8 copy.73
  349.6 0.8 collective-permute-start.7
  350.4 1.5 collective-permute-start.8
  352.0 1.2 collective-permute-done.7
  353.2 1.2 collective-permute-done.8
  354.4 1.2 collective-permute-start.10
  355.8 4.3 %collective-permute-start.12 = (bf16[64,256]{1,0:T(8,128)(2,1)S(1)}, bf16[64,256]{1,0:T(8,128)(2,1)S(1)}, u32[]{:S(2)}, u32[]{:S(2)}) collective-permute-start(bf16[64,256]{1,0:T(8,128)(2,1)S(1)} %fusion.12), channel_id=1, source_target_pairs={{0,12},{4,16},{8,20},{12,24},{16,28},{20,0},{24,4},{28,8},{1,13},{... | collective-permute-start | bytes 98312 | tf_op jit(solution)/shard_map/ppermute | solution.py:173
  360.4 2.6 collective-permute-start.14
  363.1 2.4 collective-permute-start.15
  365.4 1.5 collective-permute-start.16
  367.0 2.3 collective-permute-done.16
  369.3 0.7 convert_add_fusion.3
  370.0 1.2 copy-done.5
  371.2 16.8 %shard_map.80 = bf16[4,16,128,256]{3,2,1,0:T(8,128)(2,1)} custom-call(s32[8]{0:T(128)S(1)} %reshape.416.orb_ref, s32[8,16]{1,0:T(8,128)S(1)} %get-tuple-element.11.match_ref, bf16[8,16,128,256]{3,2,1,0:T(8,128)(2,1)} %all-to-all-done.left_ref.source_ref, bf16[8,256,256]{2,1,0:T(8,128)(2,1)S(1)} %copy-done.5, f32[4,16,128,256]{3,2,1,0:T(8,128)} %shard_map.78.start_ref), custom_call_target="tpu_custom_call" | custom-call | flops 2147483648 | bytes 25165824 | tf_op jit(solution)/shard_map/pallas_call | solution.py:139
  (122 shorter events, 16.0 us)
Async XLA Ops:
  7.2 228.7 %copy-start = (f32[32]{0:T(128)S(1)}, f32[32]{0:T(128)}, u32[]{:S(2)}) copy-start(f32[32]{0:T(128)} %param.10) | copy-start | bytes 388
  32.5 193.1 %all-to-all-start.1 = ((bf16[8,16,128,256]{3,2,1,0:T(8,128)(2,1)}), bf16[8,16,128,256]{3,2,1,0:T(8,128)(2,1)}, u32[]{:S(2)}, u32[]{:S(2)}) async-start(bf16[8,16,128,256]{3,2,1,0:T(8,128)(2,1)} %gather_fusion.15), calls=%async_computation.1 | async-start | bytes 16777216 | tf_op jit(solution)/shard_map/all_to_all | solution.py:239
  38.1 180.6 %collective-permute-start = (bf16[4,16,128,256]{3,2,1,0:T(8,128)(2,1)}, bf16[4,16,128,256]{3,2,1,0:T(8,128)(2,1)}, u32[]{:S(2)}, u32[]{:S(2)}) collective-permute-start(bf16[4,16,128,256]{3,2,1,0:T(8,128)(2,1)} %right_ref.3), channel_id=1, source_target_pairs={{0,16},{4,20},{8,24},{12,28},{16,0},{20,4},{24,8},{28,12},{1,17},{... | collective-permute-start | bytes 12582920 | tf_op jit(solution)/shard_map/ppermute | solution.py:249
  225.5 92.3 %all-to-all-start = ((bf16[8,16,128,256]{3,2,1,0:T(8,128)(2,1)}), bf16[8,16,128,256]{3,2,1,0:T(8,128)(2,1)}, u32[]{:S(2)}, u32[]{:S(2)}) async-start(bf16[8,16,128,256]{3,2,1,0:T(8,128)(2,1)} %gather_fusion.8), calls=%async_computation | async-start | bytes 16777216 | tf_op jit(solution)/shard_map/all_to_all | solution.py:239
  231.2 57.7 %all-gather.4.cloned.1.call-start = ((), (), s32[]{:S(2)}) async-start(), calls=%async_computation.2 | async-start | bytes 1310720 | tf_op jit(solution)/shard_map/all_gather | solution.py:191
  241.8 2.2 copy-start.2
  244.0 16.5 %copy-start.6 = (f32[256]{0:T(256)S(1)}, f32[256]{0:T(256)}, u32[]{:S(2)}) copy-start(f32[256]{0:T(256)} %param.11) | copy-start | bytes 3076
  257.1 7.9 %collective-permute-start.1 = (bf16[2,256,256]{1,2,0:T(8,128)(2,1)S(1)}, bf16[2,256,256]{1,2,0:T(8,128)(2,1)S(1)}, u32[]{:S(2)}, u32[]{:S(2)}) collective-permute-start(bf16[2,256,256]{1,2,0:T(8,128)(2,1)S(1)} %bitcast.115), channel_id=1, source_target_pairs={{0,1},{1,2},{2,3},{3,0},{4,5},{5,6},{6,7},{7,4},{8,9},{9,10},{10,1... | collective-permute-start | bytes 786440 | tf_op jit(solution)/shard_map/ppermute | solution.py:165
  257.3 9.2 %collective-permute-start.2 = (bf16[2,256,256]{1,2,0:T(8,128)(2,1)S(1)}, bf16[2,256,256]{1,2,0:T(8,128)(2,1)S(1)}, u32[]{:S(2)}, u32[]{:S(2)}) collective-permute-start(bf16[2,256,256]{1,2,0:T(8,128)(2,1)S(1)} %bitcast.116), channel_id=1, source_target_pairs={{0,2},{1,3},{2,0},{3,1},{4,6},{5,7},{6,4},{7,5},{8,10},{9,11},{10,... | collective-permute-start | bytes 786440 | tf_op jit(solution)/shard_map/ppermute | solution.py:165
  259.0 11.4 %collective-permute-start.3 = (bf16[2,256,256]{1,2,0:T(8,128)(2,1)S(1)}, bf16[2,256,256]{1,2,0:T(8,128)(2,1)S(1)}, u32[]{:S(2)}, u32[]{:S(2)}) collective-permute-start(bf16[2,256,256]{1,2,0:T(8,128)(2,1)S(1)} %bitcast.117), channel_id=1, source_target_pairs={{0,3},{1,0},{2,1},{3,2},{4,7},{5,4},{6,5},{7,6},{8,11},{9,8},{10,9... | collective-permute-start | bytes 786440 | tf_op jit(solution)/shard_map/ppermute | solution.py:165
  271.6 98.4 %all-gather.6.cloned.1.call-start = ((), (), s32[]{:S(2)}) async-start(), calls=%async_computation.3 | async-start | bytes 1310720 | tf_op jit(solution)/shard_map/all_gather | solution.py:191
  288.9 1.2 copy-start.4
  317.9 2.2 copy-start.3
  332.9 8.0 %collective-permute-start.4 = (bf16[2,256,256]{2,1,0:T(8,128)(2,1)S(1)}, bf16[2,256,256]{2,1,0:T(8,128)(2,1)S(1)}, u32[]{:S(2)}, u32[]{:S(2)}) collective-permute-start(bf16[2,256,256]{2,1,0:T(8,128)(2,1)S(1)} %get-tuple-element.20), channel_id=1, source_target_pairs={{0,1},{1,2},{2,3},{3,0},{4,5},{5,6},{6,7},{7,4},{8,9},{9,10},{10,1... | collective-permute-start | bytes 786440 | tf_op jit(solution)/shard_map/ppermute | solution.py:165
  333.0 9.2 %collective-permute-start.5 = (bf16[2,256,256]{2,1,0:T(8,128)(2,1)S(1)}, bf16[2,256,256]{2,1,0:T(8,128)(2,1)S(1)}, u32[]{:S(2)}, u32[]{:S(2)}) collective-permute-start(bf16[2,256,256]{2,1,0:T(8,128)(2,1)S(1)} %get-tuple-element.22), channel_id=1, source_target_pairs={{0,2},{1,3},{2,0},{3,1},{4,6},{5,7},{6,4},{7,5},{8,10},{9,11},{10,... | collective-permute-start | bytes 786440 | tf_op jit(solution)/shard_map/ppermute | solution.py:165
  334.6 11.7 %collective-permute-start.6 = (bf16[2,256,256]{2,1,0:T(8,128)(2,1)S(1)}, bf16[2,256,256]{2,1,0:T(8,128)(2,1)S(1)}, u32[]{:S(2)}, u32[]{:S(2)}) collective-permute-start(bf16[2,256,256]{2,1,0:T(8,128)(2,1)S(1)} %get-tuple-element.21), channel_id=1, source_target_pairs={{0,3},{1,0},{2,1},{3,2},{4,7},{5,4},{6,5},{7,6},{8,11},{9,8},{10,9... | collective-permute-start | bytes 786440 | tf_op jit(solution)/shard_map/ppermute | solution.py:165
  349.6 3.6 collective-permute-start.7
  350.4 3.9 collective-permute-start.8
  352.0 2.4 collective-permute-start.9
  354.4 8.7 %collective-permute-start.10 = (bf16[64,256]{1,0:T(8,128)(2,1)S(1)}, bf16[64,256]{1,0:T(8,128)(2,1)S(1)}, u32[]{:S(2)}, u32[]{:S(2)}) collective-permute-start(bf16[64,256]{1,0:T(8,128)(2,1)S(1)} %fusion.12), channel_id=1, source_target_pairs={{0,4},{4,8},{8,12},{12,16},{16,20},{20,24},{24,28},{28,0},{1,5},{5... | collective-permute-start | bytes 98312 | tf_op jit(solution)/shard_map/ppermute | solution.py:173
  355.6 9.8 %collective-permute-start.11 = (bf16[64,256]{1,0:T(8,128)(2,1)S(1)}, bf16[64,256]{1,0:T(8,128)(2,1)S(1)}, u32[]{:S(2)}, u32[]{:S(2)}) collective-permute-start(bf16[64,256]{1,0:T(8,128)(2,1)S(1)} %fusion.12), channel_id=1, source_target_pairs={{0,8},{4,12},{8,16},{12,20},{16,24},{20,28},{24,0},{28,4},{1,9},{5... | collective-permute-start | bytes 98312 | tf_op jit(solution)/shard_map/ppermute | solution.py:173
  355.8 11.1 %collective-permute-start.12 = (bf16[64,256]{1,0:T(8,128)(2,1)S(1)}, bf16[64,256]{1,0:T(8,128)(2,1)S(1)}, u32[]{:S(2)}, u32[]{:S(2)}) collective-permute-start(bf16[64,256]{1,0:T(8,128)(2,1)S(1)} %fusion.12), channel_id=1, source_target_pairs={{0,12},{4,16},{8,20},{12,24},{16,28},{20,0},{24,4},{28,8},{1,13},{... | collective-permute-start | bytes 98312 | tf_op jit(solution)/shard_map/ppermute | solution.py:173
  360.1 6.8 %collective-permute-start.13 = (bf16[64,256]{1,0:T(8,128)(2,1)S(1)}, bf16[64,256]{1,0:T(8,128)(2,1)S(1)}, u32[]{:S(2)}, u32[]{:S(2)}) collective-permute-start(bf16[64,256]{1,0:T(8,128)(2,1)S(1)} %fusion.12), channel_id=1, source_target_pairs={{0,16},{4,20},{8,24},{12,28},{16,0},{20,4},{24,8},{28,12},{1,17},{... | collective-permute-start | bytes 98312 | tf_op jit(solution)/shard_map/ppermute | solution.py:173
  360.4 6.5 %collective-permute-start.14 = (bf16[64,256]{1,0:T(8,128)(2,1)S(1)}, bf16[64,256]{1,0:T(8,128)(2,1)S(1)}, u32[]{:S(2)}, u32[]{:S(2)}) collective-permute-start(bf16[64,256]{1,0:T(8,128)(2,1)S(1)} %fusion.12), channel_id=1, source_target_pairs={{0,20},{4,24},{8,28},{12,0},{16,4},{20,8},{24,12},{28,16},{1,21},{... | collective-permute-start | bytes 98312 | tf_op jit(solution)/shard_map/ppermute | solution.py:173
  363.1 4.0 %collective-permute-start.15 = (bf16[64,256]{1,0:T(8,128)(2,1)S(1)}, bf16[64,256]{1,0:T(8,128)(2,1)S(1)}, u32[]{:S(2)}, u32[]{:S(2)}) collective-permute-start(bf16[64,256]{1,0:T(8,128)(2,1)S(1)} %fusion.12), channel_id=1, source_target_pairs={{0,24},{4,28},{8,0},{12,4},{16,8},{20,12},{24,16},{28,20},{1,25},{... | collective-permute-start | bytes 98312 | tf_op jit(solution)/shard_map/ppermute | solution.py:173
  365.4 3.9 collective-permute-start.16
  370.0 18.0 %copy-start.1 = (f32[32]{0:T(128)S(1)}, f32[32]{0:T(128)}, u32[]{:S(2)}) copy-start(f32[32]{0:T(128)} %param.10) | copy-start | bytes 388
  370.0 1.2 copy-start.5
Sparse Core Ops, SparseCore 0:
  271.7 17.0 all-gather.3
  347.7 17.5 all-gather.5

commit v3 on v2

v3 whole, which is shorter than its diff:
```python
import jax
import jax.numpy as jnp
from jax import lax
from jax.experimental import pallas as pl
from jax.experimental.pallas import tpu as pltpu
from jax.sharding import PartitionSpec as P

CHUNK_TILES = 4


def slot_match(wanted_ids, source_ids):
    same = (wanted_ids[:, :, None] == source_ids[:, None, :]) & (wanted_ids[:, :, None] >= 0)
    slots = jnp.arange(source_ids.shape[1], dtype=jnp.int32)
    return jnp.max(jnp.where(same, slots[None, None, :], -1), axis=2).astype(jnp.int32)


def gather_tiles(match_ref, row, source_ref, rows_ref):
    slot_count = source_ref.shape[1]
    for slot in range(slot_count):
        found = match_ref[row, slot]

        @pl.when(found >= 0)
        def _():
            rows_ref[slot] = source_ref[0, found]

        @pl.when(found < 0)
        def _():
            rows_ref[slot] = jnp.zeros(rows_ref.shape[1:], rows_ref.dtype)


def coulomb_kernel(orb_ref, match_ref, remote_ref, flipped_ref, out_ref, rows_ref):
    slot_count, tile_rows, width = rows_ref.shape
    gather_tiles(match_ref, pl.program_id(0), remote_ref, rows_ref)
    out_ref[0] = jnp.dot(
        flipped_ref[0],
        rows_ref[...].reshape(slot_count * tile_rows, width),
        preferred_element_type=jnp.float32,
    ).astype(out_ref.dtype)


def coulomb_call(orbitals, match, remote, flipped):
    term_count, slot_count, tile_rows, width = remote.shape
    return pl.pallas_call(
        coulomb_kernel,
        grid_spec=pltpu.PrefetchScalarGridSpec(
            num_scalar_prefetch=2,
            grid=(term_count,),
            in_specs=[
                pl.BlockSpec((1, slot_count, tile_rows, width), lambda t, orb, m: (t, 0, 0, 0)),
                pl.BlockSpec((1, width, slot_count * tile_rows), lambda t, orb, m: (orb[t], 0, 0)),
            ],
            out_specs=pl.BlockSpec((1, width, width), lambda t, orb, m: (t, 0, 0)),
            scratch_shapes=[pltpu.VMEM((slot_count, tile_rows, width), remote.dtype)],
        ),
        out_shape=jax.ShapeDtypeStruct((term_count, width, width), jnp.bfloat16),
        compiler_params=pltpu.CompilerParams(vmem_limit_bytes=56 << 20),
        cost_estimate=pl.CostEstimate(
            flops=2 * term_count * slot_count * tile_rows * width * width,
            bytes_accessed=4 * term_count * slot_count * tile_rows * width,
            transcendentals=0,
        ),
    )(orbitals, match, remote, flipped)


def add_terms(orb_ref, match_ref, source_ref, weight_ref, total_ref, rows_ref):
    term = pl.program_id(0)
    slot_count, tile_rows, width = rows_ref.shape
    gather_tiles(match_ref, term, source_ref, rows_ref)
    chunk = min(CHUNK_TILES, slot_count)
    orb = orb_ref[term]

    @pl.loop(0, slot_count // chunk)
    def _(step):
        first = step * chunk
        rows = rows_ref[pl.ds(first, chunk)].reshape(chunk * tile_rows, width)
        product = lax.dot_general(
            rows,
            weight_ref[0],
            (((1,), (1,)), ((), ())),
            preferred_element_type=jnp.float32,
        )
        total_ref[orb, pl.ds(first, chunk)] += product.reshape(chunk, tile_rows, width)


def first_gamma_kernel(orb_ref, match_ref, source_ref, weight_ref, total_ref, rows_ref):
    @pl.when(pl.program_id(0) == 0)
    def _():
        total_ref[...] = jnp.zeros_like(total_ref)

    add_terms(orb_ref, match_ref, source_ref, weight_ref, total_ref, rows_ref)


def next_gamma_kernel(
    orb_ref, match_ref, source_ref, weight_ref, start_ref, out_ref, rows_ref, total_ref, sem
):
    @pl.when(pl.program_id(0) == 0)
    def _():
        load = pltpu.make_async_copy(start_ref, total_ref, sem)
        load.start()
        load.wait()

    add_terms(orb_ref, match_ref, source_ref, weight_ref, total_ref, rows_ref)

    @pl.when(pl.program_id(0) == pl.num_programs(0) - 1)
    def _():
        out_ref[...] = total_ref[...].astype(out_ref.dtype)


def gamma_call(orbitals, match, source, weights, start, orb_count, out_type):
    term_count, slot_count, tile_rows, width = source.shape
    total_shape = (orb_count, slot_count, tile_rows, width)
    in_specs = [
        pl.BlockSpec((1, slot_count, tile_rows, width), lambda t, orb, m: (t, 0, 0, 0)),
        pl.BlockSpec((1, width, width), lambda t, orb, m: (t, 0, 0)),
    ]
    scratch = [pltpu.VMEM((slot_count, tile_rows, width), source.dtype)]
    operands = [orbitals, match, source, weights]
    if start is None:
        body = first_gamma_kernel
    else:
        body = next_gamma_kernel
        in_specs.append(pl.BlockSpec(memory_space=pl.ANY))
        scratch += [pltpu.VMEM(total_shape, jnp.float32), pltpu.SemaphoreType.DMA]
        operands.append(start)
    return pl.pallas_call(
        body,
        grid_spec=pltpu.PrefetchScalarGridSpec(
            num_scalar_prefetch=2,
            grid=(term_count,),
            in_specs=in_specs,
            out_specs=pl.BlockSpec(
                total_shape, lambda t, orb, m: (0, 0, 0, 0), pipeline_mode=pl.Buffered(1)
            ),
            scratch_shapes=scratch,
        ),
        out_shape=jax.ShapeDtypeStruct(total_shape, out_type),
        compiler_params=pltpu.CompilerParams(vmem_limit_bytes=56 << 20),
        cost_estimate=pl.CostEstimate(
            flops=2 * term_count * slot_count * tile_rows * width * width,
            bytes_accessed=2 * term_count * slot_count * tile_rows * width
            + 8 * orb_count * slot_count * tile_rows * width,
            transcendentals=0,
        ),
    )(*operands)


def exchange(blocks, axis):
    count = lax.axis_size(axis)
    me = lax.axis_index(axis)
    arrived = [lax.dynamic_index_in_dim(blocks, me, 0, keepdims=False)]
    for shift in range(1, count):
        block = lax.dynamic_index_in_dim(blocks, lax.rem(me + shift, count), 0, keepdims=False)
        arrived.append(lax.ppermute(block, axis, [(d, (d + shift) % count) for d in range(count)]))
    return arrived


def pair_weights(partial, energy_pair, vir_energy, counted):
    group_count = lax.axis_size("aux")
    share = lax.axis_index("aux")
    term_count, width = partial.shape[:2]
    share_terms = term_count // group_count
    parts = exchange(partial.reshape(group_count, share_terms, width, width), "aux")
    coulomb = parts[0].astype(jnp.float32)
    for part in parts[1:]:
        coulomb = coulomb + part.astype(jnp.float32)
    energy = lax.dynamic_slice_in_dim(energy_pair, share * share_terms, share_terms, 0)
    denominator = energy[:, None, None] - vir_energy[None, :, None] - vir_energy[None, None, :]
    amplitude = coulomb / denominator
    mixed = 2.0 * amplitude - jnp.swapaxes(amplitude, 1, 2)
    weights = lax.all_gather(mixed.astype(jnp.bfloat16), "aux", axis=0, tiled=True)
    if counted is None:
        return weights
    amplitude, mixed = amplitude[counted], mixed[counted]
    density = jnp.einsum(
        "rac,rbc->ab", amplitude, mixed, precision=lax.Precision.HIGHEST
    ) + jnp.einsum("rca,rcb->ab", amplitude, mixed, precision=lax.Precision.HIGHEST)
    return weights, density


def per_device(int_tiles, tile_ids, tile_counts, pair_list, occ_energy, vir_energy):
    peer_count = lax.axis_size("occ")
    group_count = lax.axis_size("aux")
    orb_count, slot_count, tile_rows, width = int_tiles.shape
    assert pair_list.shape[0] == peer_count and peer_count % 2 == 0
    half = peer_count // 2
    assert half % group_count == 0
    me = lax.axis_index("occ")

    slot_range = jnp.arange(slot_count, dtype=jnp.int32)
    live_ids = jnp.where(slot_range[None, :] < tile_counts, tile_ids, -1)
    packed = jnp.concatenate([pair_list.reshape(-1), live_ids.reshape(-1)])
    everyone = lax.all_gather(packed, "occ")
    everyone, own_tiles = lax.optimization_barrier((everyone, int_tiles))
    all_pairs = everyone[:, : 2 * peer_count].reshape(peer_count, peer_count, 2)
    all_ids = everyone[:, 2 * peer_count :].reshape(peer_count * orb_count, slot_count)

    near = me // half * half + jnp.arange(half, dtype=jnp.int32)
    far = lax.rem(near + half, peer_count)
    partner = lax.rem(me + half, peer_count)

    def wanted_of(owner):
        return jnp.stack([all_pairs[owner, near, 0], all_pairs[near, owner, 1]], axis=1)

    def terms_of(peers):
        remote = jnp.stack([all_pairs[peers, me, 0], all_pairs[me, peers, 1]], axis=1)
        own = jnp.stack([all_pairs[peers, me, 1], all_pairs[me, peers, 0]], axis=1)
        remote = peers[:, None] * orb_count + remote
        match = slot_match(live_ids[own.reshape(-1)], all_ids[remote.reshape(-1)])
        energy_pair = occ_energy[remote] + occ_energy[me * orb_count + own]
        return own, match.reshape(half, 2, slot_count), energy_pair

    groups = [list(range(half)), list(range(half, peer_count))]

    def near_exchange(tiles):
        return lax.all_to_all(
            tiles, "occ", split_axis=0, concat_axis=0, axis_index_groups=groups, tiled=True
        )

    swapped = [(d, (d + half) % peer_count) for d in range(peer_count)]
    partner_tiles = lax.ppermute(own_tiles, "occ", swapped)
    near_tiles = near_exchange(own_tiles[wanted_of(me).reshape(-1)])
    flipped = int_tiles.reshape(orb_count, slot_count * tile_rows, width).swapaxes(1, 2)

    own, match, energy_pair = terms_of(near)
    own, match = own.reshape(-1), match.reshape(-1, slot_count)
    partial = coulomb_call(own, match, near_tiles, flipped)
    partner_tiles, partial = lax.optimization_barrier((partner_tiles, partial))

    wanted = wanted_of(partner)
    first_tiles = near_exchange(partner_tiles[wanted[:, 0]])
    first_tiles, second_tiles = lax.optimization_barrier((first_tiles, partner_tiles[wanted[:, 1]]))
    second_tiles = near_exchange(second_tiles)

    weights, density = pair_weights(
        partial, energy_pair.reshape(-1), vir_energy, slice(None, None, 2)
    )
    gamma = gamma_call(own, match, near_tiles, weights, None, orb_count, jnp.float32)

    own, match, energy_pair = terms_of(far)
    partial = coulomb_call(own[:, 0], match[:, 0], first_tiles, flipped)
    weights, more_density = pair_weights(partial, energy_pair[:, 0], vir_energy, slice(None))
    gamma = gamma_call(own[:, 0], match[:, 0], first_tiles, weights, gamma, orb_count, jnp.float32)

    density = (density + more_density).astype(jnp.bfloat16)
    parts = exchange(density.reshape(group_count, width // group_count, width), "aux")
    density = parts[0].astype(jnp.float32)
    for part in parts[1:]:
        density = density + part.astype(jnp.float32)
    block = density.astype(jnp.bfloat16)
    for shift in range(1, half):
        turned = [(d, d // half * half + (d + shift) % half) for d in range(peer_count)]
        density = density + lax.ppermute(block, "occ", turned).astype(jnp.float32)

    second_tiles, gamma = lax.optimization_barrier((second_tiles, gamma))
    partial = coulomb_call(own[:, 1], match[:, 1], second_tiles, flipped)
    weights = pair_weights(partial, energy_pair[:, 1], vir_energy, None)
    weights, density = lax.optimization_barrier((weights, density))
    density = density + lax.ppermute(density.astype(jnp.bfloat16), "occ", swapped).astype(jnp.float32)
    gamma = gamma_call(own[:, 1], match[:, 1], second_tiles, weights, gamma, orb_count, jnp.bfloat16)
    return gamma, density


def solution(mesh):
    placed = (
        P("occ", "aux", None, None),
        P("occ", "aux"),
        P("occ", "aux"),
        P("occ", None),
        P(),
        P(),
    )
    return jax.shard_map(
        per_device,
        mesh=mesh,
        in_specs=placed,
        out_specs=(P("occ", "aux", None, None), P("aux", None)),
        check_vma=False,
    )
```

time: 396 us -> 424 us (1.071)
  blocking collectives: 13.1 us -> 28 us
  waiting for transfers between devices: 232 us -> 221 us
  Pallas kernels: 57.5 us -> 67.9 us
  local copies, waits for them, and re-layouts: 37.7 us -> 44 us
    all_to_all x2 -> x3, waiting for transfers between devices: 12.7 us -> 205 us  [near_exchange(): lax.all_to_all(tiles, 'occ', split_axis=0, concat_axis=0, axis_index_grou...]
    ppermute x1, waiting for transfers between devices: 179 us -> 0.01 us  [per_device(): partner_tiles = lax.ppermute(own_tiles, 'occ', swapped)]
    all_gather x0 -> x2, blocking collectives: none -> 15 us  [pair_weights(): lax.all_gather(mixed.astype(jnp.bfloat16), 'aux', axis=0, tiled=True)]
    all_gather x2 -> x1, waiting for transfers between devices: 16.7 us -> 2.32 us  [pair_weights(): lax.all_gather(mixed.astype(jnp.bfloat16), 'aux', axis=0, tiled=True)]
    pallas_call x2 -> x3, Pallas kernels: 31.8 us -> 43.7 us  [gamma_call(): pl.pallas_call(body, grid_spec=pltpu.PrefetchScalarGridSpec(num_scalar_pr...]
    ppermute x9 -> x12, waiting for transfers between devices: 22 us -> 14.1 us  [exchange(): lax.ppermute(block, axis, [(d, (d + shift) % count) for d in range(count)])]
    unnamed x18 -> x16, local copies, waits for them, and re-layouts: 8.98 us -> 2.17 us
    reshape x6 -> x5, local copies, waits for them, and re-layouts: 0.51 us -> 7.19 us  [the longest x1 6.26 us: per_device(): int_tiles.reshape(orb_count, slot_count * tile_rows, width).swapaxes(1, 2)]
  transfers between devices with their start and end apart: 21 -> 21, of which waited for: 13 -> 9; matrix products, arithmetic and copies ran while one was open for 6% -> 8% of each run, Pallas kernels for 7% -> 16%
where the time goes in v3:
time: 424 us; the launch traced here: 423 us
  waiting for transfers between devices  221 us (52%)
  Pallas kernels  67.9 us (16%)
  local copies, waits for them, and re-layouts  44 us (10%)
  starting transfers between devices  36.7 us (9%)
  blocking collectives  28 us (7%)
  between operations  15.2 us (4%)
  other arithmetic  7.6 us (2%)
    all_to_all x3, waiting for transfers between devices, near_exchange(): lax.all_to_all(tiles, 'occ', split_axis=0, concat_axis=0, axis_index_grou...  205 us
    pallas_call x3, Pallas kernels, gamma_call(): pl.pallas_call(body, grid_spec=pltpu.PrefetchScalarGridSpec(num_scalar_pr...  43.7 us
    pallas_call x3, Pallas kernels, coulomb_call(): pl.pallas_call(coulomb_kernel, grid_spec=pltpu.PrefetchScalarGridSpec(num...  24.2 us
    all_to_all x3, starting transfers between devices, near_exchange(): lax.all_to_all(tiles, 'occ', split_axis=0, concat_axis=0, axis_index_grou...  15.4 us
    all_gather x2, blocking collectives, pair_weights(): lax.all_gather(mixed.astype(jnp.bfloat16), 'aux', axis=0, tiled=True)  15 us
    ppermute x12, waiting for transfers between devices, exchange(): lax.ppermute(block, axis, [(d, (d + shift) % count) for d in range(count)])  14.1 us
    unnamed x1, blocking collectives  13.1 us
    ppermute x12, starting transfers between devices, exchange(): lax.ppermute(block, axis, [(d, (d + shift) % count) for d in range(count)])  10.7 us
  transfers between devices with their start and end apart: 21, of which 9 were waited for; matrix products, arithmetic and copies ran while one was open for 8% of the time, Pallas kernels for 16%

profile of v3, /device:TPU:0, one launch (start us, length us, event | category | flops | bytes accessed | tf_op | source)
XLA Modules:
  0.0 422.7 jit_solution(10862574226526590065)
XLA Ops:
  7.2 0.8 fusion.18
  8.1 0.8 copy.76
  8.9 1.2 dynamic-slice.17
  11.0 13.1 %all-reduce = s32[640]{0:T(1024)S(1)} all-reduce(s32[640]{0:T(1024)S(1)} %add_dynamic-update-slice_fusion), channel_id=2, replica_groups=mesh['occ'=8,'aux'=4] {'occ'}, use_global_device_ids=true, to_apply=%add | all-reduce | flops 640 | bytes 5120
  24.2 0.7 gather_fusion.7
  25.7 6.8 %gather_fusion.12 = bf16[8,16,128,256]{3,2,1,0:T(8,128)(2,1)} fusion(bf16[4,16,128,256]{3,2,1,0:T(8,128)(2,1)} %param.6, s32[1024]{0:T(1024)S(1)} %pad_clamp_fusion.6), kind=kCustom, calls=%fused_computation.12 | custom fusion | bytes 16777248 | tf_op jit(solution)/shard_map/gather | solution.py:221
  32.5 5.7 %all-to-all-start = ((bf16[8,16,128,256]{3,2,1,0:T(8,128)(2,1)}), bf16[8,16,128,256]{3,2,1,0:T(8,128)(2,1)}, u32[]{:S(2)}, u32[]{:S(2)}) async-start(bf16[8,16,128,256]{3,2,1,0:T(8,128)(2,1)} %gather_fusion.12), calls=%async_computation | async-start | bytes 16777216 | tf_op jit(solution)/shard_map/all_to_all | solution.py:215
  38.7 0.7 reshape.668.orb_ref
  40.2 0.7 gather_fusion
  42.2 0.7 gather_fusion.4
  45.9 6.3 %copy.98 = bf16[4,2048,256]{1,2,0:T(8,128)(2,1)} copy(bf16[4,2048,256]{2,1,0:T(8,128)(2,1)} %bitcast.143) | data formatting | bytes 8388608 | tf_op jit(solution)/shard_map/reshape | solution.py:222
  52.7 0.9 select_reduce_fusion.match_ref
  53.6 163.0 %all-to-all-done.remote_ref.source_ref = bf16[8,16,128,256]{3,2,1,0:T(8,128)(2,1)} async-done(((bf16[8,16,128,256]{3,2,1,0:T(8,128)(2,1)}), bf16[8,16,128,256]{3,2,1,0:T(8,128)(2,1)}, u32[]{:S(2)}, u32[]{:S(2)}) %all-to-all-start) | async-done | bytes 8388640 | tf_op jit(solution)/shard_map/all_to_all | solution.py:215
  216.6 11.0 %shard_map.77 = bf16[8,256,256]{2,1,0:T(8,128)(2,1)} custom-call(s32[8]{0:T(128)} %reshape.668.orb_ref, s32[8,16]{1,0:T(8,128)} %select_reduce_fusion.match_ref, bf16[8,16,128,256]{3,2,1,0:T(8,128)(2,1)} %all-to-all-done.remote_ref.source_ref, bf16[4,256,2048]{2,1,0:T(8,128)(2,1)} %bitcast.140), custom_call_target="tpu_custom_call" | custom-call | flops 2147483648 | bytes 16777216 | tf_op jit(solution)/shard_map/pallas_call | solution.py:43
  227.7 5.0 %gather_fusion.14 = bf16[4,16,128,256]{3,2,1,0:T(8,128)(2,1)} fusion(bf16[4,16,128,256]{3,2,1,0:T(8,128)(2,1)} %collective-permute-done, s32[1024]{0:T(1024)S(1)} %pad_clamp_fusion.5), kind=kCustom, calls=%fused_computation.14 | custom fusion | bytes 8388624 | tf_op jit(solution)/shard_map/gather | solution.py:230
  232.7 4.9 %all-to-all-start.1 = ((bf16[4,16,128,256]{3,2,1,0:T(8,128)(2,1)}), bf16[4,16,128,256]{3,2,1,0:T(8,128)(2,1)}, u32[]{:S(2)}, u32[]{:S(2)}) async-start(bf16[4,16,128,256]{3,2,1,0:T(8,128)(2,1)} %gather_fusion.14), calls=%async_computation.1 | async-start | bytes 8388608 | tf_op jit(solution)/shard_map/all_to_all | solution.py:215
  237.6 5.0 %gather_fusion.16 = bf16[4,16,128,256]{3,2,1,0:T(8,128)(2,1)} fusion(bf16[4,16,128,256]{3,2,1,0:T(8,128)(2,1)} %collective-permute-done, s32[1024]{0:T(1024)S(1)} %pad_clamp_fusion.4), kind=kCustom, calls=%fused_computation.16 | custom fusion | bytes 8388624 | tf_op jit(solution)/shard_map/gather | solution.py:231
  242.6 41.8 %all-to-all-done.1.remote_ref.source_ref = bf16[4,16,128,256]{3,2,1,0:T(8,128)(2,1)} async-done(((bf16[4,16,128,256]{3,2,1,0:T(8,128)(2,1)}), bf16[4,16,128,256]{3,2,1,0:T(8,128)(2,1)}, u32[]{:S(2)}, u32[]{:S(2)}) %all-to-all-start.1) | async-done | bytes 4194336 | tf_op jit(solution)/shard_map/all_to_all | solution.py:215
  284.4 4.9 %all-to-all-start.2 = ((bf16[4,16,128,256]{3,2,1,0:T(8,128)(2,1)}), bf16[4,16,128,256]{3,2,1,0:T(8,128)(2,1)}, u32[]{:S(2)}, u32[]{:S(2)}) async-start(bf16[4,16,128,256]{3,2,1,0:T(8,128)(2,1)} %gather_fusion.16), calls=%async_computation.2 | async-start | bytes 8388608 | tf_op jit(solution)/shard_map/all_to_all | solution.py:215
  292.4 1.6 collective-permute-start.5
  294.0 1.4 collective-permute-start.6
  297.6 2.8 collective-permute-done.4
  300.4 1.2 collective-permute-done.5
  301.6 4.1 collective-permute-done.6
  306.1 0.8 fusion.36
  308.4 1.3 broadcast_subtract_fusion.1
  311.3 6.7 %shard_map.78 = bf16[4,256,256]{2,1,0:T(8,128)(2,1)} custom-call(s32[4]{0:T(128)} %copy-done.4, s32[4,16]{1,0:T(4,128)} %bitcast.152, bf16[4,16,128,256]{3,2,1,0:T(8,128)(2,1)} %all-to-all-done.1.remote_ref.source_ref, bf16[4,256,2048]{2,1,0:T(8,128)(2,1)} %bitcast.141), custom_call_target="tpu_custom_call" | custom-call | flops 1073741824 | bytes 8388608 | tf_op jit(solution)/shard_map/pallas_call | solution.py:43
  317.9 1.1 constant_dynamic-slice_fusion.11
  319.0 1.2 collective-permute-start.1
  320.2 1.2 collective-permute-start.3
  321.9 2.3 all-gather.3.cloned.1.call-done.weight_ref
  324.2 16.2 %shard_map.79.start_ref = f32[4,16,128,256]{3,2,1,0:T(8,128)} custom-call(s32[8]{0:T(128)} %reshape.668.orb_ref, s32[8,16]{1,0:T(8,128)} %select_reduce_fusion.match_ref, bf16[8,16,128,256]{3,2,1,0:T(8,128)(2,1)} %all-to-all-done.remote_ref.source_ref, bf16[8,256,256]{2,1,0:T(8,128)(2,1)} %all-gather.3.cloned.1.call-done.weight_ref), custom_call_target="tpu_custom_call" | custom-call | flops 2147483648 | bytes 25165824 | tf_op jit(solution)/shard_map/pallas_call | solution.py:125
  340.4 1.0 subtract_divide_fusion.1
  343.1 1.4 collective-permute-start.12
  344.9 8.0 %all_gather.17.weight_ref = bf16[4,256,256]{2,1,0:T(8,128)(2,1)} all-gather(bf16[1,256,256]{2,1,0:T(8,128)(2,1)S(1)} %copy.88), channel_id=1, replica_groups=mesh['occ'=8,'aux'=4] {'aux'}, dimensions={0}, use_global_device_ids=true | all-gather | bytes 655360 | tf_op jit(solution)/shard_map/all_gather | solution.py:170
  352.9 14.4 %shard_map.80.start_ref = f32[4,16,128,256]{3,2,1,0:T(8,128)} custom-call(s32[4]{0:T(128)} %copy-done.4, s32[4,16]{1,0:T(4,128)} %bitcast.153, bf16[4,16,128,256]{3,2,1,0:T(8,128)(2,1)} %all-to-all-done.1.remote_ref.source_ref, bf16[4,256,256]{2,1,0:T(8,128)(2,1)} %all_gather.17.weight_ref, f32[4,16,128,256]{3,2,1,0:T(8,128)} %shard_map.79.start_ref), custom_call_target="tpu_custom_call" | custom-call | flops 1073741824 | bytes 20971520 | tf_op jit(solution)/shard_map/pallas_call | solution.py:125
  367.4 2.5 collective-permute-start.15
  371.0 6.5 %shard_map.81 = bf16[4,256,256]{2,1,0:T(8,128)(2,1)} custom-call(s32[4]{0:T(128)} %copy-done.5, s32[4,16]{1,0:T(4,128)} %bitcast.154, bf16[4,16,128,256]{3,2,1,0:T(8,128)(2,1)} %all-to-all-done.2.remote_ref.source_ref, bf16[4,256,2048]{2,1,0:T(8,128)(2,1)} %bitcast.142), custom_call_target="tpu_custom_call" | custom-call | flops 1073741824 | bytes 8388608 | tf_op jit(solution)/shard_map/pallas_call | solution.py:43
  377.5 1.1 constant_dynamic-slice_fusion.3
  378.6 1.7 collective-permute-start.9
  380.3 0.8 collective-permute-start.8
  381.2 2.0 collective-permute-done.7
  383.2 0.9 collective-permute-done.9
  384.1 3.1 collective-permute-done.8
  387.2 1.0 subtract_divide_fusion
  388.5 7.0 %all_gather.19.weight_ref = bf16[4,256,256]{2,1,0:T(8,128)(2,1)} all-gather(bf16[1,256,256]{2,1,0:T(8,128)(2,1)S(1)} %copy.97), channel_id=1, replica_groups=mesh['occ'=8,'aux'=4] {'aux'}, dimensions={0}, use_global_device_ids=true | all-gather | bytes 655360 | tf_op jit(solution)/shard_map/all_gather | solution.py:170
  395.5 6.6 %collective-permute-start.16 = (bf16[64,256]{1,0:T(8,128)(2,1)S(1)}, bf16[64,256]{1,0:T(8,128)(2,1)S(1)}, u32[]{:S(2)}, u32[]{:S(2)}) collective-permute-start(bf16[64,256]{1,0:T(8,128)(2,1)S(1)} %convert_element_type.114), channel_id=1, source_target_pairs={{0,16},{4,20},{8,24},{12,28},{16,0},{20,4},{24,8},{28,12},{1,17},{... | collective-permute-start | bytes 98312 | tf_op jit(solution)/shard_map/ppermute | solution.py:258
  402.1 13.2 %shard_map.82 = bf16[4,16,128,256]{3,2,1,0:T(8,128)(2,1)} custom-call(s32[4]{0:T(128)} %copy-done.5, s32[4,16]{1,0:T(4,128)} %bitcast.155, bf16[4,16,128,256]{3,2,1,0:T(8,128)(2,1)} %all-to-all-done.2.remote_ref.source_ref, bf16[4,256,256]{2,1,0:T(8,128)(2,1)} %all_gather.19.weight_ref, f32[4,16,128,256]{3,2,1,0:T(8,128)} %shard_map.80.start_ref), custom_call_target="tpu_custom_call" | custom-call | flops 1073741824 | bytes 20971520 | tf_op jit(solution)/shard_map/pallas_call | solution.py:125
  (142 shorter events, 20.8 us)
Async XLA Ops:
  7.2 283.2 %copy-start = (f32[32]{0:T(128)S(1)}, f32[32]{0:T(128)}, u32[]{:S(2)}) copy-start(f32[32]{0:T(128)} %param.10) | copy-start | bytes 388
  32.5 184.1 %all-to-all-start = ((bf16[8,16,128,256]{3,2,1,0:T(8,128)(2,1)}), bf16[8,16,128,256]{3,2,1,0:T(8,128)(2,1)}, u32[]{:S(2)}, u32[]{:S(2)}) async-start(bf16[8,16,128,256]{3,2,1,0:T(8,128)(2,1)} %gather_fusion.12), calls=%async_computation | async-start | bytes 16777216 | tf_op jit(solution)/shard_map/all_to_all | solution.py:215
  38.2 189.4 %collective-permute-start = (bf16[4,16,128,256]{3,2,1,0:T(8,128)(2,1)}, bf16[4,16,128,256]{3,2,1,0:T(8,128)(2,1)}, u32[]{:S(2)}, u32[]{:S(2)}) collective-permute-start(bf16[4,16,128,256]{3,2,1,0:T(8,128)(2,1)} %param.6), channel_id=1, source_target_pairs={{0,16},{4,20},{8,24},{12,28},{16,0},{20,4},{24,8},{28,12},{1,17},{... | collective-permute-start | bytes 12582920 | tf_op jit(solution)/shard_map/ppermute | solution.py:220
  40.2 249.2 %copy-start.4 = (s32[4]{0:T(128)}, s32[4]{0:T(128)S(1)}, u32[]{:S(2)}) copy-start(s32[4]{0:T(128)S(1)} %gather_fusion.1) | copy-start | bytes 52
  40.8 248.6 %copy-start.5 = (s32[4]{0:T(128)}, s32[4]{0:T(128)S(1)}, u32[]{:S(2)}) copy-start(s32[4]{0:T(128)S(1)} %gather_fusion) | copy-start | bytes 52
  232.7 51.7 %all-to-all-start.1 = ((bf16[4,16,128,256]{3,2,1,0:T(8,128)(2,1)}), bf16[4,16,128,256]{3,2,1,0:T(8,128)(2,1)}, u32[]{:S(2)}, u32[]{:S(2)}) async-start(bf16[4,16,128,256]{3,2,1,0:T(8,128)(2,1)} %gather_fusion.14), calls=%async_computation.1 | async-start | bytes 8388608 | tf_op jit(solution)/shard_map/all_to_all | solution.py:215
  284.4 86.6 %all-to-all-start.2 = ((bf16[4,16,128,256]{3,2,1,0:T(8,128)(2,1)}), bf16[4,16,128,256]{3,2,1,0:T(8,128)(2,1)}, u32[]{:S(2)}, u32[]{:S(2)}) async-start(bf16[4,16,128,256]{3,2,1,0:T(8,128)(2,1)} %gather_fusion.16), calls=%async_computation.2 | async-start | bytes 8388608 | tf_op jit(solution)/shard_map/all_to_all | solution.py:215
  289.3 2.5 copy-start.3
  289.3 2.6 copy-start.2
  289.3 34.9 %all-gather.3.cloned.1.call-start = ((), (), s32[]{:S(2)}) async-start(), calls=%async_computation.3 | async-start | bytes 1310720 | tf_op jit(solution)/shard_map/all_gather | solution.py:170
  292.4 8.0 %collective-permute-start.4 = (bf16[2,256,256]{1,2,0:T(8,128)(2,1)S(1)}, bf16[2,256,256]{1,2,0:T(8,128)(2,1)S(1)}, u32[]{:S(2)}, u32[]{:S(2)}) collective-permute-start(bf16[2,256,256]{1,2,0:T(8,128)(2,1)S(1)} %bitcast.150), channel_id=1, source_target_pairs={{0,1},{1,2},{2,3},{3,0},{4,5},{5,6},{6,7},{7,4},{8,9},{9,10},{10,1... | collective-permute-start | bytes 786440 | tf_op jit(solution)/shard_map/ppermute | solution.py:153
  292.4 9.2 %collective-permute-start.5 = (bf16[2,256,256]{1,2,0:T(8,128)(2,1)S(1)}, bf16[2,256,256]{1,2,0:T(8,128)(2,1)S(1)}, u32[]{:S(2)}, u32[]{:S(2)}) collective-permute-start(bf16[2,256,256]{1,2,0:T(8,128)(2,1)S(1)} %bitcast.149), channel_id=1, source_target_pairs={{0,2},{1,3},{2,0},{3,1},{4,6},{5,7},{6,4},{7,5},{8,10},{9,11},{10,... | collective-permute-start | bytes 786440 | tf_op jit(solution)/shard_map/ppermute | solution.py:153
  294.0 11.7 %collective-permute-start.6 = (bf16[2,256,256]{1,2,0:T(8,128)(2,1)S(1)}, bf16[2,256,256]{1,2,0:T(8,128)(2,1)S(1)}, u32[]{:S(2)}, u32[]{:S(2)}) collective-permute-start(bf16[2,256,256]{1,2,0:T(8,128)(2,1)S(1)} %bitcast.148), channel_id=1, source_target_pairs={{0,3},{1,0},{2,1},{3,2},{4,7},{5,4},{6,5},{7,6},{8,11},{9,8},{10,9... | collective-permute-start | bytes 786440 | tf_op jit(solution)/shard_map/ppermute | solution.py:153
  319.0 21.4 %collective-permute-start.1 = (bf16[1,256,256]{2,1,0:T(8,128)(2,1)S(1)}, bf16[1,256,256]{2,1,0:T(8,128)(2,1)S(1)}, u32[]{:S(2)}, u32[]{:S(2)}) collective-permute-start(bf16[1,256,256]{2,1,0:T(8,128)(2,1)S(1)} %get-tuple-element.33), channel_id=1, source_target_pairs={{0,1},{1,2},{2,3},{3,0},{4,5},{5,6},{6,7},{7,4},{8,9},{9,10},{10,1... | collective-permute-start | bytes 393224 | tf_op jit(solution)/shard_map/ppermute | solution.py:153
  320.2 20.2 %collective-permute-start.3 = (bf16[1,256,256]{2,1,0:T(8,128)(2,1)S(1)}, bf16[1,256,256]{2,1,0:T(8,128)(2,1)S(1)}, u32[]{:S(2)}, u32[]{:S(2)}) collective-permute-start(bf16[1,256,256]{2,1,0:T(8,128)(2,1)S(1)} %get-tuple-element.34), channel_id=1, source_target_pairs={{0,3},{1,0},{2,1},{3,2},{4,7},{5,4},{6,5},{7,6},{8,11},{9,8},{10,9... | collective-permute-start | bytes 393224 | tf_op jit(solution)/shard_map/ppermute | solution.py:153
  321.4 19.0 %collective-permute-start.2 = (bf16[1,256,256]{2,1,0:T(8,128)(2,1)S(1)}, bf16[1,256,256]{2,1,0:T(8,128)(2,1)S(1)}, u32[]{:S(2)}, u32[]{:S(2)}) collective-permute-start(bf16[1,256,256]{2,1,0:T(8,128)(2,1)S(1)} %get-tuple-element.35), channel_id=1, source_target_pairs={{0,2},{1,3},{2,0},{3,1},{4,6},{5,7},{6,4},{7,5},{8,10},{9,11},{10,... | collective-permute-start | bytes 393224 | tf_op jit(solution)/shard_map/ppermute | solution.py:153
  342.8 24.6 %collective-permute-start.10 = (bf16[64,256]{1,0:T(8,128)(2,1)S(1)}, bf16[64,256]{1,0:T(8,128)(2,1)S(1)}, u32[]{:S(2)}, u32[]{:S(2)}) collective-permute-start(bf16[64,256]{1,0:T(8,128)(2,1)S(1)} %get-tuple-element.36), channel_id=1, source_target_pairs={{0,1},{1,2},{2,3},{3,0},{4,5},{5,6},{6,7},{7,4},{8,9},{9,10},{10,1... | collective-permute-start | bytes 98312 | tf_op jit(solution)/shard_map/ppermute | solution.py:153
  343.1 24.2 %collective-permute-start.12 = (bf16[64,256]{1,0:T(8,128)(2,1)S(1)}, bf16[64,256]{1,0:T(8,128)(2,1)S(1)}, u32[]{:S(2)}, u32[]{:S(2)}) collective-permute-start(bf16[64,256]{1,0:T(8,128)(2,1)S(1)} %get-tuple-element.37), channel_id=1, source_target_pairs={{0,3},{1,0},{2,1},{3,2},{4,7},{5,4},{6,5},{7,6},{8,11},{9,8},{10,9... | collective-permute-start | bytes 98312 | tf_op jit(solution)/shard_map/ppermute | solution.py:153
  344.5 22.8 %collective-permute-start.11 = (bf16[64,256]{1,0:T(8,128)(2,1)S(1)}, bf16[64,256]{1,0:T(8,128)(2,1)S(1)}, u32[]{:S(2)}, u32[]{:S(2)}) collective-permute-start(bf16[64,256]{1,0:T(8,128)(2,1)S(1)} %get-tuple-element.38), channel_id=1, source_target_pairs={{0,2},{1,3},{2,0},{3,1},{4,6},{5,7},{6,4},{7,5},{8,10},{9,11},{10,... | collective-permute-start | bytes 98312 | tf_op jit(solution)/shard_map/ppermute | solution.py:153
  367.4 13.0 %collective-permute-start.15 = (bf16[64,256]{1,0:T(8,128)(2,1)S(1)}, bf16[64,256]{1,0:T(8,128)(2,1)S(1)}, u32[]{:S(2)}, u32[]{:S(2)}) collective-permute-start(bf16[64,256]{1,0:T(8,128)(2,1)S(1)} %fusion.17), channel_id=1, source_target_pairs={{0,12},{4,0},{8,4},{12,8},{16,28},{20,16},{24,20},{28,24},{1,13},{... | collective-permute-start | bytes 98312 | tf_op jit(solution)/shard_map/ppermute | solution.py:252
  369.8 11.3 %collective-permute-start.14 = (bf16[64,256]{1,0:T(8,128)(2,1)S(1)}, bf16[64,256]{1,0:T(8,128)(2,1)S(1)}, u32[]{:S(2)}, u32[]{:S(2)}) collective-permute-start(bf16[64,256]{1,0:T(8,128)(2,1)S(1)} %fusion.17), channel_id=1, source_target_pairs={{0,8},{4,12},{8,0},{12,4},{16,24},{20,28},{24,16},{28,20},{1,9},{5... | collective-permute-start | bytes 98312 | tf_op jit(solution)/shard_map/ppermute | solution.py:252
  370.4 10.8 %collective-permute-start.13 = (bf16[64,256]{1,0:T(8,128)(2,1)S(1)}, bf16[64,256]{1,0:T(8,128)(2,1)S(1)}, u32[]{:S(2)}, u32[]{:S(2)}) collective-permute-start(bf16[64,256]{1,0:T(8,128)(2,1)S(1)} %fusion.17), channel_id=1, source_target_pairs={{0,4},{4,8},{8,12},{12,0},{16,20},{20,24},{24,28},{28,16},{1,5},{5... | collective-permute-start | bytes 98312 | tf_op jit(solution)/shard_map/ppermute | solution.py:252
  378.5 4.7 %collective-permute-start.7 = (bf16[1,256,256]{2,1,0:T(8,128)(2,1)S(1)}, bf16[1,256,256]{2,1,0:T(8,128)(2,1)S(1)}, u32[]{:S(2)}, u32[]{:S(2)}) collective-permute-start(bf16[1,256,256]{2,1,0:T(8,128)(2,1)S(1)} %get-tuple-element.30), channel_id=1, source_target_pairs={{0,1},{1,2},{2,3},{3,0},{4,5},{5,6},{6,7},{7,4},{8,9},{9,10},{10,1... | collective-permute-start | bytes 393224 | tf_op jit(solution)/shard_map/ppermute | solution.py:153
  378.6 5.5 %collective-permute-start.9 = (bf16[1,256,256]{2,1,0:T(8,128)(2,1)S(1)}, bf16[1,256,256]{2,1,0:T(8,128)(2,1)S(1)}, u32[]{:S(2)}, u32[]{:S(2)}) collective-permute-start(bf16[1,256,256]{2,1,0:T(8,128)(2,1)S(1)} %get-tuple-element.31), channel_id=1, source_target_pairs={{0,3},{1,0},{2,1},{3,2},{4,7},{5,4},{6,5},{7,6},{8,11},{9,8},{10,9... | collective-permute-start | bytes 393224 | tf_op jit(solution)/shard_map/ppermute | solution.py:153
  380.3 6.9 %collective-permute-start.8 = (bf16[1,256,256]{2,1,0:T(8,128)(2,1)S(1)}, bf16[1,256,256]{2,1,0:T(8,128)(2,1)S(1)}, u32[]{:S(2)}, u32[]{:S(2)}) collective-permute-start(bf16[1,256,256]{2,1,0:T(8,128)(2,1)S(1)} %get-tuple-element.32), channel_id=1, source_target_pairs={{0,2},{1,3},{2,0},{3,1},{4,6},{5,7},{6,4},{7,5},{8,10},{9,11},{10,... | collective-permute-start | bytes 393224 | tf_op jit(solution)/shard_map/ppermute | solution.py:153
  395.5 19.8 %collective-permute-start.16 = (bf16[64,256]{1,0:T(8,128)(2,1)S(1)}, bf16[64,256]{1,0:T(8,128)(2,1)S(1)}, u32[]{:S(2)}, u32[]{:S(2)}) collective-permute-start(bf16[64,256]{1,0:T(8,128)(2,1)S(1)} %convert_element_type.114), channel_id=1, source_target_pairs={{0,16},{4,20},{8,24},{12,28},{16,0},{20,4},{24,8},{28,12},{1,17},{... | collective-permute-start | bytes 98312 | tf_op jit(solution)/shard_map/ppermute | solution.py:258
  402.1 13.8 %copy-start.1 = (f32[32]{0:T(128)S(1)}, f32[32]{0:T(128)}, u32[]{:S(2)}) copy-start(f32[32]{0:T(128)} %param.10) | copy-start | bytes 388
Sparse Core Ops, SparseCore 0:
  307.0 17.1 all-gather.2

commit v4 on v3

--- a/solution.py
+++ b/solution.py
@@ -1,3 +1,4 @@
+import functools
 import jax
 import jax.numpy as jnp
 from jax import lax
@@ -82,12 +83,20 @@
         total_ref[orb, pl.ds(first, chunk)] += product.reshape(chunk, tile_rows, width)
 
 
-def first_gamma_kernel(orb_ref, match_ref, source_ref, weight_ref, total_ref, rows_ref):
+def first_gamma_kernel(
+    counts, orb_ref, match_ref, near_ref, near_weight, far_ref, far_weight, total_ref, rows_ref
+):
     @pl.when(pl.program_id(0) == 0)
     def _():
         total_ref[...] = jnp.zeros_like(total_ref)
 
-    add_terms(orb_ref, match_ref, source_ref, weight_ref, total_ref, rows_ref)
+    @pl.when(pl.program_id(0) < counts)
+    def _():
+        add_terms(orb_ref, match_ref, near_ref, near_weight, total_ref, rows_ref)
+
+    @pl.when(pl.program_id(0) >= counts)
+    def _():
+        add_terms(orb_ref, match_ref, far_ref, far_weight, total_ref, rows_ref)
 
 
 def next_gamma_kernel(
@@ -106,17 +115,28 @@
         out_ref[...] = total_ref[...].astype(out_ref.dtype)
 
 
-def gamma_call(orbitals, match, source, weights, start, orb_count, out_type):
-    term_count, slot_count, tile_rows, width = source.shape
+def gamma_call(orbitals, match, sources, start, orb_count, out_type):
+    slot_count, tile_rows, width = sources[0][0].shape[1:]
     total_shape = (orb_count, slot_count, tile_rows, width)
-    in_specs = [
-        pl.BlockSpec((1, slot_count, tile_rows, width), lambda t, orb, m: (t, 0, 0, 0)),
-        pl.BlockSpec((1, width, width), lambda t, orb, m: (t, 0, 0)),
-    ]
-    scratch = [pltpu.VMEM((slot_count, tile_rows, width), source.dtype)]
-    operands = [orbitals, match, source, weights]
+    in_specs, operands, first = [], [orbitals, match], 0
+    for tiles, weights in sources:
+        last = tiles.shape[0] - 1
+
+        def place(t, first=first, last=last):
+            return jnp.clip(t - first, 0, last)
+
+        in_specs += [
+            pl.BlockSpec(
+                (1, slot_count, tile_rows, width),
+                lambda t, orb, m, place=place: (place(t), 0, 0, 0),
+            ),
+            pl.BlockSpec((1, width, width), lambda t, orb, m, place=place: (place(t), 0, 0)),
+        ]
+        operands += [tiles, weights]
+        first += tiles.shape[0]
+    scratch = [pltpu.VMEM((slot_count, tile_rows, width), sources[0][0].dtype)]
     if start is None:
-        body = first_gamma_kernel
+        body = functools.partial(first_gamma_kernel, sources[0][0].shape[0])
     else:
         body = next_gamma_kernel
         in_specs.append(pl.BlockSpec(memory_space=pl.ANY))
@@ -126,7 +146,7 @@
         body,
         grid_spec=pltpu.PrefetchScalarGridSpec(
             num_scalar_prefetch=2,
-            grid=(term_count,),
+            grid=(first,),
             in_specs=in_specs,
             out_specs=pl.BlockSpec(
                 total_shape, lambda t, orb, m: (0, 0, 0, 0), pipeline_mode=pl.Buffered(1)
@@ -136,8 +156,8 @@
         out_shape=jax.ShapeDtypeStruct(total_shape, out_type),
         compiler_params=pltpu.CompilerParams(vmem_limit_bytes=56 << 20),
         cost_estimate=pl.CostEstimate(
-            flops=2 * term_count * slot_count * tile_rows * width * width,
-            bytes_accessed=2 * term_count * slot_count * tile_rows * width
+            flops=2 * first * slot_count * tile_rows * width * width,
+            bytes_accessed=2 * first * slot_count * tile_rows * width
             + 8 * orb_count * slot_count * tile_rows * width,
             transcendentals=0,
         ),
@@ -218,45 +238,52 @@
 
     swapped = [(d, (d + half) % peer_count) for d in range(peer_count)]
     partner_tiles = lax.ppermute(own_tiles, "occ", swapped)
+    flipped = own_tiles.reshape(orb_count, slot_count * tile_rows, width).swapaxes(1, 2)
     near_tiles = near_exchange(own_tiles[wanted_of(me).reshape(-1)])
-    flipped = int_tiles.reshape(orb_count, slot_count * tile_rows, width).swapaxes(1, 2)
-
-    own, match, energy_pair = terms_of(near)
-    own, match = own.reshape(-1), match.reshape(-1, slot_count)
-    partial = coulomb_call(own, match, near_tiles, flipped)
-    partner_tiles, partial = lax.optimization_barrier((partner_tiles, partial))
 
     wanted = wanted_of(partner)
     first_tiles = near_exchange(partner_tiles[wanted[:, 0]])
-    first_tiles, second_tiles = lax.optimization_barrier((first_tiles, partner_tiles[wanted[:, 1]]))
+    near_tiles, partner_tiles = lax.optimization_barrier((near_tiles, partner_tiles))
+    near_own, near_match, energy_pair = terms_of(near)
+    near_own, near_match = near_own.reshape(-1), near_match.reshape(-1, slot_count)
+    partial = coulomb_call(near_own, near_match, near_tiles, flipped)
+    near_weights, density = pair_weights(
+        partial, energy_pair.reshape(-1), vir_energy, slice(None, None, 2)
+    )
+
+    second_tiles, first_tiles, near_weights, density = lax.optimization_barrier(
+        (partner_tiles[wanted[:, 1]], first_tiles, near_weights, density)
+    )
     second_tiles = near_exchange(second_tiles)
-
-    weights, density = pair_weights(
-        partial, energy_pair.reshape(-1), vir_energy, slice(None, None, 2)
-    )
-    gamma = gamma_call(own, match, near_tiles, weights, None, orb_count, jnp.float32)
-
     own, match, energy_pair = terms_of(far)
     partial = coulomb_call(own[:, 0], match[:, 0], first_tiles, flipped)
-    weights, more_density = pair_weights(partial, energy_pair[:, 0], vir_energy, slice(None))
-    gamma = gamma_call(own[:, 0], match[:, 0], first_tiles, weights, gamma, orb_count, jnp.float32)
+    first_weights, more_density = pair_weights(partial, energy_pair[:, 0], vir_energy, slice(None))
 
     density = (density + more_density).astype(jnp.bfloat16)
     parts = exchange(density.reshape(group_count, width // group_count, width), "aux")
     density = parts[0].astype(jnp.float32)
     for part in parts[1:]:
         density = density + part.astype(jnp.float32)
+    density = density + lax.ppermute(density.astype(jnp.bfloat16), "occ", swapped).astype(jnp.float32)
     block = density.astype(jnp.bfloat16)
     for shift in range(1, half):
         turned = [(d, d // half * half + (d + shift) % half) for d in range(peer_count)]
         density = density + lax.ppermute(block, "occ", turned).astype(jnp.float32)
 
+    gamma = gamma_call(
+        jnp.concatenate([near_own, own[:, 0]]),
+        jnp.concatenate([near_match, match[:, 0]]),
+        [(near_tiles, near_weights), (first_tiles, first_weights)],
+        None,
+        orb_count,
+        jnp.float32,
+    )
     second_tiles, gamma = lax.optimization_barrier((second_tiles, gamma))
     partial = coulomb_call(own[:, 1], match[:, 1], second_tiles, flipped)
     weights = pair_weights(partial, energy_pair[:, 1], vir_energy, None)
-    weights, density = lax.optimization_barrier((weights, density))
-    density = density + lax.ppermute(density.astype(jnp.bfloat16), "occ", swapped).astype(jnp.float32)
-    gamma = gamma_call(own[:, 1], match[:, 1], second_tiles, weights, gamma, orb_count, jnp.bfloat16)
+    gamma = gamma_call(
+        own[:, 1], match[:, 1], [(second_tiles, weights)], gamma, orb_count, jnp.bfloat16
+    )
     return gamma, density
 
 

time: 424 us -> 402 us (0.948)
  waiting for transfers between devices: 221 us -> 209 us
  Pallas kernels: 67.9 us -> 60.1 us
    all_to_all x3, waiting for transfers between devices: 205 us -> 0.01 us  [near_exchange(): lax.all_to_all(tiles, 'occ', split_axis=0, concat_axis=0, axis_index_grou...]
    ppermute x1, waiting for transfers between devices: 0.01 us -> 180 us  [per_device(): partner_tiles = lax.ppermute(own_tiles, 'occ', swapped)]
    pallas_call x3 -> x2, Pallas kernels: 43.7 us -> 35.3 us  [gamma_call(): pl.pallas_call(body, grid_spec=pltpu.PrefetchScalarGridSpec(num_scalar_pr...]
    all_gather x1, waiting for transfers between devices: 2.32 us -> 10 us  [pair_weights(): lax.all_gather(mixed.astype(jnp.bfloat16), 'aux', axis=0, tiled=True)]
    ppermute x12, waiting for transfers between devices: 14.1 us -> 19.4 us  [exchange(): lax.ppermute(block, axis, [(d, (d + shift) % count) for d in range(count)])]
    ppermute x1, starting transfers between devices: 6.59 us -> 2.25 us  [per_device(): lax.ppermute(density.astype(jnp.bfloat16), 'occ', swapped)]
  transfers between devices with their start and end apart: 21 -> 21, of which waited for: 9 -> 10; matrix products, arithmetic and copies ran while one was open for 8% -> 10% of each run, Pallas kernels for 16% -> 12%
where the time goes in v4:
time: 402 us; the launch traced here: 401 us
  waiting for transfers between devices  209 us (52%)
  Pallas kernels  60.1 us (15%)
  local copies, waits for them, and re-layouts  45.1 us (11%)
  starting transfers between devices  32.6 us (8%)
  blocking collectives  27.8 us (7%)
  between operations  15.2 us (4%)
  other arithmetic  8.78 us (2%)
    ppermute x1, waiting for transfers between devices, per_device(): partner_tiles = lax.ppermute(own_tiles, 'occ', swapped)  180 us
    pallas_call x2, Pallas kernels, gamma_call(): pl.pallas_call(body, grid_spec=pltpu.PrefetchScalarGridSpec(num_scalar_pr...  35.3 us
    pallas_call x3, Pallas kernels, coulomb_call(): pl.pallas_call(coulomb_kernel, grid_spec=pltpu.PrefetchScalarGridSpec(num...  24.8 us
    ppermute x12, waiting for transfers between devices, exchange(): lax.ppermute(block, axis, [(d, (d + shift) % count) for d in range(count)])  19.4 us
    all_to_all x3, starting transfers between devices, near_exchange(): lax.all_to_all(tiles, 'occ', split_axis=0, concat_axis=0, axis_index_grou...  15.3 us
    all_gather x2, blocking collectives, pair_weights(): lax.all_gather(mixed.astype(jnp.bfloat16), 'aux', axis=0, tiled=True)  14.7 us
    unnamed x1, blocking collectives  13.1 us
    all_gather x1, waiting for transfers between devices, pair_weights(): lax.all_gather(mixed.astype(jnp.bfloat16), 'aux', axis=0, tiled=True)  10 us
  transfers between devices with their start and end apart: 21, of which 10 were waited for; matrix products, arithmetic and copies ran while one was open for 10% of the time, Pallas kernels for 12%

profile of v4, /device:TPU:0, one launch (start us, length us, event | category | flops | bytes accessed | tf_op | source)
XLA Modules:
  0.0 400.5 jit_solution(1162465012266538440)
XLA Ops:
  7.3 0.8 fusion.16
  8.1 0.8 copy.76
  9.0 1.2 dynamic-slice.17
  11.1 13.1 %all-reduce = s32[640]{0:T(1024)S(1)} all-reduce(s32[640]{0:T(1024)S(1)} %add_dynamic-update-slice_fusion), channel_id=2, replica_groups=mesh['occ'=8,'aux'=4] {'occ'}, use_global_device_ids=true, to_apply=%add | all-reduce | flops 640 | bytes 5120
  24.3 0.7 gather_fusion.1
  24.9 0.7 gather_fusion
  25.6 0.7 gather_fusion.7
  27.1 6.9 %gather_fusion.8 = bf16[8,16,128,256]{3,2,1,0:T(8,128)(2,1)} fusion(bf16[4,16,128,256]{3,2,1,0:T(8,128)(2,1)} %param.6, s32[1024]{0:T(1024)S(1)} %pad_clamp_fusion.8), kind=kCustom, calls=%fused_computation.8 | custom fusion | bytes 16777248 | tf_op jit(solution)/shard_map/gather | solution.py:242
  34.0 5.7 %all-to-all-start = ((bf16[8,16,128,256]{3,2,1,0:T(8,128)(2,1)}), bf16[8,16,128,256]{3,2,1,0:T(8,128)(2,1)}, u32[]{:S(2)}, u32[]{:S(2)}) async-start(bf16[8,16,128,256]{3,2,1,0:T(8,128)(2,1)} %gather_fusion.8), calls=%async_computation | async-start | bytes 16777216 | tf_op jit(solution)/shard_map/all_to_all | solution.py:235
  40.7 179.6 %collective-permute-done = bf16[4,16,128,256]{3,2,1,0:T(8,128)(2,1)} collective-permute-done((bf16[4,16,128,256]{3,2,1,0:T(8,128)(2,1)}, bf16[4,16,128,256]{3,2,1,0:T(8,128)(2,1)}, u32[]{:S(2)}, u32[]{:S(2)}) %collective-permute-start) | collective-permute-done | bytes 4194336 | tf_op jit(solution)/shard_map/ppermute | solution.py:240
  220.3 5.0 %gather_fusion.12 = bf16[4,16,128,256]{3,2,1,0:T(8,128)(2,1)} fusion(bf16[4,16,128,256]{3,2,1,0:T(8,128)(2,1)} %collective-permute-done, s32[1024]{0:T(1024)S(1)} %pad_clamp_fusion.6), kind=kCustom, calls=%fused_computation.12 | custom fusion | bytes 8388624 | tf_op jit(solution)/shard_map/gather | solution.py:245
  225.3 4.8 %all-to-all-start.1 = ((bf16[4,16,128,256]{3,2,1,0:T(8,128)(2,1)}), bf16[4,16,128,256]{3,2,1,0:T(8,128)(2,1)}, u32[]{:S(2)}, u32[]{:S(2)}) async-start(bf16[4,16,128,256]{3,2,1,0:T(8,128)(2,1)} %gather_fusion.12), calls=%async_computation.1 | async-start | bytes 8388608 | tf_op jit(solution)/shard_map/all_to_all | solution.py:235
  235.1 6.3 %copy.98 = bf16[4,2048,256]{1,2,0:T(8,128)(2,1)} copy(bf16[4,2048,256]{2,1,0:T(8,128)(2,1)} %bitcast.140) | data formatting | bytes 8388608 | tf_op jit(solution)/shard_map/reshape | solution.py:241
  242.0 0.9 select_reduce_fusion.match_ref
  242.9 11.5 %shard_map.77 = bf16[8,256,256]{2,1,0:T(8,128)(2,1)} custom-call(s32[8]{0:T(128)} %reshape.666.orb_ref, s32[8,16]{1,0:T(8,128)} %select_reduce_fusion.match_ref, bf16[8,16,128,256]{3,2,1,0:T(8,128)(2,1)} %all-to-all-done.remote_ref.near_ref, bf16[4,256,2048]{2,1,0:T(8,128)(2,1)} %bitcast.137), custom_call_target="tpu_custom_call" | custom-call | flops 2147483648 | bytes 16777216 | tf_op jit(solution)/shard_map/pallas_call | solution.py:44
  254.4 1.3 constant_dynamic-slice_fusion.11
  256.2 1.6 collective-permute-start.2
  257.8 1.4 collective-permute-start.3
  260.8 3.4 collective-permute-done.1
  264.2 1.2 collective-permute-done.2
  265.4 4.1 %collective-permute-done.3 = bf16[2,256,256]{1,2,0:T(8,128)(2,1)S(1)} collective-permute-done((bf16[2,256,256]{1,2,0:T(8,128)(2,1)S(1)}, bf16[2,256,256]{1,2,0:T(8,128)(2,1)S(1)}, u32[]{:S(2)}, u32[]{:S(2)}) %collective-permute-start.3) | collective-permute-done | bytes 262176 | tf_op jit(solution)/shard_map/ppermute | solution.py:173
  269.8 0.8 fusion.36
  271.3 5.0 %gather_fusion.10 = bf16[4,16,128,256]{3,2,1,0:T(8,128)(2,1)} fusion(bf16[4,16,128,256]{3,2,1,0:T(8,128)(2,1)} %collective-permute-done, s32[1024]{0:T(1024)S(1)} %pad_clamp_fusion.7), kind=kCustom, calls=%fused_computation.10 | custom fusion | bytes 8388624 | tf_op jit(solution)/shard_map/gather | solution.py:255
  277.3 10.0 %all-gather.3.cloned.1.call-done.near_weight = bf16[8,256,256]{2,1,0:T(8,128)(2,1)} async-done(((bf16[2,256,256]{2,1,0:T(8,128)(2,1)}), bf16[8,256,256]{2,1,0:T(8,128)(2,1)}) %all-gather.3.cloned.1.call-update) | async-done | bytes 1048592 | tf_op jit(solution)/shard_map/all_gather | solution.py:190
  287.4 4.8 %all-to-all-start.2 = ((bf16[4,16,128,256]{3,2,1,0:T(8,128)(2,1)}), bf16[4,16,128,256]{3,2,1,0:T(8,128)(2,1)}, u32[]{:S(2)}, u32[]{:S(2)}) async-start(bf16[4,16,128,256]{3,2,1,0:T(8,128)(2,1)} %gather_fusion.10), calls=%async_computation.2 | async-start | bytes 8388608 | tf_op jit(solution)/shard_map/all_to_all | solution.py:235
  296.3 1.2 broadcast_subtract_fusion.1
  298.1 6.7 %shard_map.78 = bf16[4,256,256]{2,1,0:T(8,128)(2,1)} custom-call(s32[4]{0:T(128)} %copy-done.5, s32[4,16]{1,0:T(4,128)} %bitcast.148, bf16[4,16,128,256]{3,2,1,0:T(8,128)(2,1)} %all-to-all-done.1.remote_ref.far_ref, bf16[4,256,2048]{2,1,0:T(8,128)(2,1)} %bitcast.138), custom_call_target="tpu_custom_call" | custom-call | flops 1073741824 | bytes 8388608 | tf_op jit(solution)/shard_map/pallas_call | solution.py:44
  304.8 1.1 constant_dynamic-slice_fusion.7
  306.1 1.5 collective-permute-start.6
  309.2 1.9 collective-permute-done.4
  311.1 3.4 collective-permute-done.5
  314.5 1.0 subtract_divide_fusion.1
  316.9 1.7 collective-permute-start.12
  319.0 7.8 %all_gather.18.far_weight = bf16[4,256,256]{2,1,0:T(8,128)(2,1)} all-gather(bf16[1,256,256]{2,1,0:T(8,128)(2,1)S(1)} %copy.95), channel_id=1, replica_groups=mesh['occ'=8,'aux'=4] {'aux'}, dimensions={0}, use_global_device_ids=true | all-gather | bytes 655360 | tf_op jit(solution)/shard_map/all_gather | solution.py:190
  326.8 2.2 collective-permute-start.13
  329.1 22.2 %shard_map.79.start_ref = f32[4,16,128,256]{3,2,1,0:T(8,128)} custom-call(s32[12]{0:T(128)} %pad_add_fusion.4.orb_ref, s32[12,16]{1,0:T(8,128)} %pad_add_fusion.match_ref, bf16[8,16,128,256]{3,2,1,0:T(8,128)(2,1)} %all-to-all-done.remote_ref.near_ref, bf16[8,256,256]{2,1,0:T(8,128)(2,1)} %all-gather.3.cloned.1.call-done.near_weight, ...), custom_call_target="tpu_custom_call" | custom-call | flops 3221225472 | bytes 29360128 | tf_op jit(solution)/shard_map/pallas_call | solution.py:145
  351.3 3.5 collective-permute-start.16
  356.0 6.6 %shard_map.80 = bf16[4,256,256]{2,1,0:T(8,128)(2,1)} custom-call(s32[4]{0:T(128)} %copy-done.4, s32[4,16]{1,0:T(4,128)} %bitcast.150, bf16[4,16,128,256]{3,2,1,0:T(8,128)(2,1)} %all-to-all-done.2.remote_ref.source_ref, bf16[4,256,2048]{2,1,0:T(8,128)(2,1)} %bitcast.139), custom_call_target="tpu_custom_call" | custom-call | flops 1073741824 | bytes 8388608 | tf_op jit(solution)/shard_map/pallas_call | solution.py:44
  362.6 1.1 constant_dynamic-slice_fusion.3
  363.8 1.7 collective-permute-start.9
  365.5 0.8 collective-permute-start.8
  366.3 0.7 convert_add_fusion.2
  366.9 1.5 collective-permute-done.7
  368.5 0.8 collective-permute-done.9
  369.3 3.1 collective-permute-done.8
  372.4 1.0 subtract_divide_fusion
  373.7 7.0 %all_gather.19.weight_ref = bf16[4,256,256]{2,1,0:T(8,128)(2,1)} all-gather(bf16[1,256,256]{2,1,0:T(8,128)(2,1)S(1)} %copy.97), channel_id=1, replica_groups=mesh['occ'=8,'aux'=4] {'aux'}, dimensions={0}, use_global_device_ids=true | all-gather | bytes 655360 | tf_op jit(solution)/shard_map/all_gather | solution.py:190
  380.6 13.1 %shard_map.81 = bf16[4,16,128,256]{3,2,1,0:T(8,128)(2,1)} custom-call(s32[4]{0:T(128)} %copy-done.4, s32[4,16]{1,0:T(4,128)} %bitcast.151, bf16[4,16,128,256]{3,2,1,0:T(8,128)(2,1)} %all-to-all-done.2.remote_ref.source_ref, bf16[4,256,256]{2,1,0:T(8,128)(2,1)} %all_gather.19.weight_ref, f32[4,16,128,256]{3,2,1,0:T(8,128)} %shard_map.79.start_ref), custom_call_target="tpu_custom_call" | custom-call | flops 1073741824 | bytes 20971520 | tf_op jit(solution)/shard_map/pallas_call | solution.py:145
  (148 shorter events, 21.8 us)
Async XLA Ops:
  7.2 252.0 %copy-start = (f32[32]{0:T(128)S(1)}, f32[32]{0:T(128)}, u32[]{:S(2)}) copy-start(f32[32]{0:T(128)} %param.10) | copy-start | bytes 388
  24.9 267.3 %copy-start.5 = (s32[4]{0:T(128)}, s32[4]{0:T(128)S(1)}, u32[]{:S(2)}) copy-start(s32[4]{0:T(128)S(1)} %gather_fusion.1) | copy-start | bytes 52
  25.6 266.7 %copy-start.4 = (s32[4]{0:T(128)}, s32[4]{0:T(128)S(1)}, u32[]{:S(2)}) copy-start(s32[4]{0:T(128)S(1)} %gather_fusion) | copy-start | bytes 52
  34.0 191.3 %all-to-all-start = ((bf16[8,16,128,256]{3,2,1,0:T(8,128)(2,1)}), bf16[8,16,128,256]{3,2,1,0:T(8,128)(2,1)}, u32[]{:S(2)}, u32[]{:S(2)}) async-start(bf16[8,16,128,256]{3,2,1,0:T(8,128)(2,1)} %gather_fusion.8), calls=%async_computation | async-start | bytes 16777216 | tf_op jit(solution)/shard_map/all_to_all | solution.py:235
  39.6 180.6 %collective-permute-start = (bf16[4,16,128,256]{3,2,1,0:T(8,128)(2,1)}, bf16[4,16,128,256]{3,2,1,0:T(8,128)(2,1)}, u32[]{:S(2)}, u32[]{:S(2)}) collective-permute-start(bf16[4,16,128,256]{3,2,1,0:T(8,128)(2,1)} %param.6), channel_id=1, source_target_pairs={{0,16},{4,20},{8,24},{12,28},{16,0},{20,4},{24,8},{28,12},{1,17},{... | collective-permute-start | bytes 12582920 | tf_op jit(solution)/shard_map/ppermute | solution.py:240
  225.3 52.1 %all-to-all-start.1 = ((bf16[4,16,128,256]{3,2,1,0:T(8,128)(2,1)}), bf16[4,16,128,256]{3,2,1,0:T(8,128)(2,1)}, u32[]{:S(2)}, u32[]{:S(2)}) async-start(bf16[4,16,128,256]{3,2,1,0:T(8,128)(2,1)} %gather_fusion.12), calls=%async_computation.1 | async-start | bytes 8388608 | tf_op jit(solution)/shard_map/all_to_all | solution.py:235
  230.1 57.2 %all-gather.3.cloned.1.call-start = ((), (), s32[]{:S(2)}) async-start(), calls=%async_computation.3 | async-start | bytes 1310720 | tf_op jit(solution)/shard_map/all_gather | solution.py:190
  254.4 6.1 %copy-start.2 = (f32[256]{0:T(256)S(1)}, f32[256]{0:T(256)}, u32[]{:S(2)}) copy-start(f32[256]{0:T(256)} %param.11) | copy-start | bytes 3076
  256.1 8.0 %collective-permute-start.1 = (bf16[2,256,256]{1,2,0:T(8,128)(2,1)S(1)}, bf16[2,256,256]{1,2,0:T(8,128)(2,1)S(1)}, u32[]{:S(2)}, u32[]{:S(2)}) collective-permute-start(bf16[2,256,256]{1,2,0:T(8,128)(2,1)S(1)} %bitcast.146), channel_id=1, source_target_pairs={{0,1},{1,2},{2,3},{3,0},{4,5},{5,6},{6,7},{7,4},{8,9},{9,10},{10,1... | collective-permute-start | bytes 786440 | tf_op jit(solution)/shard_map/ppermute | solution.py:173
  256.2 9.2 %collective-permute-start.2 = (bf16[2,256,256]{1,2,0:T(8,128)(2,1)S(1)}, bf16[2,256,256]{1,2,0:T(8,128)(2,1)S(1)}, u32[]{:S(2)}, u32[]{:S(2)}) collective-permute-start(bf16[2,256,256]{1,2,0:T(8,128)(2,1)S(1)} %bitcast.145), channel_id=1, source_target_pairs={{0,2},{1,3},{2,0},{3,1},{4,6},{5,7},{6,4},{7,5},{8,10},{9,11},{10,... | collective-permute-start | bytes 786440 | tf_op jit(solution)/shard_map/ppermute | solution.py:173
  257.8 11.7 %collective-permute-start.3 = (bf16[2,256,256]{1,2,0:T(8,128)(2,1)S(1)}, bf16[2,256,256]{1,2,0:T(8,128)(2,1)S(1)}, u32[]{:S(2)}, u32[]{:S(2)}) collective-permute-start(bf16[2,256,256]{1,2,0:T(8,128)(2,1)S(1)} %bitcast.144), channel_id=1, source_target_pairs={{0,3},{1,0},{2,1},{3,2},{4,7},{5,4},{6,5},{7,6},{8,11},{9,8},{10,9... | collective-permute-start | bytes 786440 | tf_op jit(solution)/shard_map/ppermute | solution.py:173
  287.4 68.7 %all-to-all-start.2 = ((bf16[4,16,128,256]{3,2,1,0:T(8,128)(2,1)}), bf16[4,16,128,256]{3,2,1,0:T(8,128)(2,1)}, u32[]{:S(2)}, u32[]{:S(2)}) async-start(bf16[4,16,128,256]{3,2,1,0:T(8,128)(2,1)} %gather_fusion.10), calls=%async_computation.2 | async-start | bytes 8388608 | tf_op jit(solution)/shard_map/all_to_all | solution.py:235
  298.1 9.9 %copy-start.6 = (s32[4]{0:T(128)S(1)}, s32[4]{0:T(128)}, u32[]{:S(2)}) copy-start(s32[4]{0:T(128)} %copy-done.5) | copy-start | bytes 52
  298.1 9.9 %copy-start.7 = (s32[8]{0:T(128)S(1)}, s32[8]{0:T(128)}, u32[]{:S(2)}) copy-start(s32[8]{0:T(128)} %reshape.666.orb_ref) | copy-start | bytes 100
  298.1 10.5 %copy-start.1 = (s32[8,16]{1,0:T(8,128)S(1)}, s32[8,16]{1,0:T(8,128)}, u32[]{:S(2)}) copy-start(s32[8,16]{1,0:T(8,128)} %select_reduce_fusion.match_ref) | copy-start | bytes 1540
  298.1 10.5 %copy-start.3 = (s32[4,1,16]{2,1,0:T(1,128)S(1)}, s32[4,1,16]{2,1,0:T(1,128)}, u32[]{:S(2)}) copy-start(s32[4,1,16]{2,1,0:T(1,128)} %get-tuple-element.41) | copy-start | bytes 772
  305.8 5.3 %collective-permute-start.4 = (bf16[1,256,256]{2,1,0:T(8,128)(2,1)S(1)}, bf16[1,256,256]{2,1,0:T(8,128)(2,1)S(1)}, u32[]{:S(2)}, u32[]{:S(2)}) collective-permute-start(bf16[1,256,256]{2,1,0:T(8,128)(2,1)S(1)} %get-tuple-element.35), channel_id=1, source_target_pairs={{0,1},{1,2},{2,3},{3,0},{4,5},{5,6},{6,7},{7,4},{8,9},{9,10},{10,1... | collective-permute-start | bytes 393224 | tf_op jit(solution)/shard_map/ppermute | solution.py:173
  306.1 5.0 %collective-permute-start.6 = (bf16[1,256,256]{2,1,0:T(8,128)(2,1)S(1)}, bf16[1,256,256]{2,1,0:T(8,128)(2,1)S(1)}, u32[]{:S(2)}, u32[]{:S(2)}) collective-permute-start(bf16[1,256,256]{2,1,0:T(8,128)(2,1)S(1)} %get-tuple-element.36), channel_id=1, source_target_pairs={{0,3},{1,0},{2,1},{3,2},{4,7},{5,4},{6,5},{7,6},{8,11},{9,8},{10,9... | collective-permute-start | bytes 393224 | tf_op jit(solution)/shard_map/ppermute | solution.py:173
  307.6 6.9 %collective-permute-start.5 = (bf16[1,256,256]{2,1,0:T(8,128)(2,1)S(1)}, bf16[1,256,256]{2,1,0:T(8,128)(2,1)S(1)}, u32[]{:S(2)}, u32[]{:S(2)}) collective-permute-start(bf16[1,256,256]{2,1,0:T(8,128)(2,1)S(1)} %get-tuple-element.37), channel_id=1, source_target_pairs={{0,2},{1,3},{2,0},{3,1},{4,6},{5,7},{6,4},{7,5},{8,10},{9,11},{10,... | collective-permute-start | bytes 393224 | tf_op jit(solution)/shard_map/ppermute | solution.py:173
  316.9 9.9 %collective-permute-start.10 = (bf16[64,256]{1,0:T(8,128)(2,1)S(1)}, bf16[64,256]{1,0:T(8,128)(2,1)S(1)}, u32[]{:S(2)}, u32[]{:S(2)}) collective-permute-start(bf16[64,256]{1,0:T(8,128)(2,1)S(1)} %get-tuple-element.38), channel_id=1, source_target_pairs={{0,1},{1,2},{2,3},{3,0},{4,5},{5,6},{6,7},{7,4},{8,9},{9,10},{10,1... | collective-permute-start | bytes 98312 | tf_op jit(solution)/shard_map/ppermute | solution.py:173
  316.9 9.9 %collective-permute-start.12 = (bf16[64,256]{1,0:T(8,128)(2,1)S(1)}, bf16[64,256]{1,0:T(8,128)(2,1)S(1)}, u32[]{:S(2)}, u32[]{:S(2)}) collective-permute-start(bf16[64,256]{1,0:T(8,128)(2,1)S(1)} %get-tuple-element.39), channel_id=1, source_target_pairs={{0,3},{1,0},{2,1},{3,2},{4,7},{5,4},{6,5},{7,6},{8,11},{9,8},{10,9... | collective-permute-start | bytes 98312 | tf_op jit(solution)/shard_map/ppermute | solution.py:173
  318.7 8.1 %collective-permute-start.11 = (bf16[64,256]{1,0:T(8,128)(2,1)S(1)}, bf16[64,256]{1,0:T(8,128)(2,1)S(1)}, u32[]{:S(2)}, u32[]{:S(2)}) collective-permute-start(bf16[64,256]{1,0:T(8,128)(2,1)S(1)} %get-tuple-element.40), channel_id=1, source_target_pairs={{0,2},{1,3},{2,0},{3,1},{4,6},{5,7},{6,4},{7,5},{8,10},{9,11},{10,... | collective-permute-start | bytes 98312 | tf_op jit(solution)/shard_map/ppermute | solution.py:173
  326.8 24.5 %collective-permute-start.13 = (bf16[64,256]{1,0:T(8,128)(2,1)S(1)}, bf16[64,256]{1,0:T(8,128)(2,1)S(1)}, u32[]{:S(2)}, u32[]{:S(2)}) collective-permute-start(bf16[64,256]{1,0:T(8,128)(2,1)S(1)} %get-tuple-element.22), channel_id=1, source_target_pairs={{0,16},{4,20},{8,24},{12,28},{16,0},{20,4},{24,8},{28,12},{1,17},{... | collective-permute-start | bytes 98312 | tf_op jit(solution)/shard_map/ppermute | solution.py:267
  351.3 14.2 %collective-permute-start.16 = (bf16[64,256]{1,0:T(8,128)(2,1)S(1)}, bf16[64,256]{1,0:T(8,128)(2,1)S(1)}, u32[]{:S(2)}, u32[]{:S(2)}) collective-permute-start(bf16[64,256]{1,0:T(8,128)(2,1)S(1)} %fusion.15), channel_id=1, source_target_pairs={{0,12},{4,0},{8,4},{12,8},{16,28},{20,16},{24,20},{28,24},{1,13},{... | collective-permute-start | bytes 98312 | tf_op jit(solution)/shard_map/ppermute | solution.py:271
  354.9 11.4 %collective-permute-start.15 = (bf16[64,256]{1,0:T(8,128)(2,1)S(1)}, bf16[64,256]{1,0:T(8,128)(2,1)S(1)}, u32[]{:S(2)}, u32[]{:S(2)}) collective-permute-start(bf16[64,256]{1,0:T(8,128)(2,1)S(1)} %fusion.15), channel_id=1, source_target_pairs={{0,8},{4,12},{8,0},{12,4},{16,24},{20,28},{24,16},{28,20},{1,9},{5... | collective-permute-start | bytes 98312 | tf_op jit(solution)/shard_map/ppermute | solution.py:271
  355.4 10.9 %collective-permute-start.14 = (bf16[64,256]{1,0:T(8,128)(2,1)S(1)}, bf16[64,256]{1,0:T(8,128)(2,1)S(1)}, u32[]{:S(2)}, u32[]{:S(2)}) collective-permute-start(bf16[64,256]{1,0:T(8,128)(2,1)S(1)} %fusion.15), channel_id=1, source_target_pairs={{0,4},{4,8},{8,12},{12,0},{16,20},{20,24},{24,28},{28,16},{1,5},{5... | collective-permute-start | bytes 98312 | tf_op jit(solution)/shard_map/ppermute | solution.py:271
  363.7 4.8 %collective-permute-start.7 = (bf16[1,256,256]{2,1,0:T(8,128)(2,1)S(1)}, bf16[1,256,256]{2,1,0:T(8,128)(2,1)S(1)}, u32[]{:S(2)}, u32[]{:S(2)}) collective-permute-start(bf16[1,256,256]{2,1,0:T(8,128)(2,1)S(1)} %get-tuple-element.32), channel_id=1, source_target_pairs={{0,1},{1,2},{2,3},{3,0},{4,5},{5,6},{6,7},{7,4},{8,9},{9,10},{10,1... | collective-permute-start | bytes 393224 | tf_op jit(solution)/shard_map/ppermute | solution.py:173
  363.8 5.5 %collective-permute-start.9 = (bf16[1,256,256]{2,1,0:T(8,128)(2,1)S(1)}, bf16[1,256,256]{2,1,0:T(8,128)(2,1)S(1)}, u32[]{:S(2)}, u32[]{:S(2)}) collective-permute-start(bf16[1,256,256]{2,1,0:T(8,128)(2,1)S(1)} %get-tuple-element.33), channel_id=1, source_target_pairs={{0,3},{1,0},{2,1},{3,2},{4,7},{5,4},{6,5},{7,6},{8,11},{9,8},{10,9... | collective-permute-start | bytes 393224 | tf_op jit(solution)/shard_map/ppermute | solution.py:173
  365.5 6.9 %collective-permute-start.8 = (bf16[1,256,256]{2,1,0:T(8,128)(2,1)S(1)}, bf16[1,256,256]{2,1,0:T(8,128)(2,1)S(1)}, u32[]{:S(2)}, u32[]{:S(2)}) collective-permute-start(bf16[1,256,256]{2,1,0:T(8,128)(2,1)S(1)} %get-tuple-element.34), channel_id=1, source_target_pairs={{0,2},{1,3},{2,0},{3,1},{4,6},{5,7},{6,4},{7,5},{8,10},{9,11},{10,... | collective-permute-start | bytes 393224 | tf_op jit(solution)/shard_map/ppermute | solution.py:173
Sparse Core Ops, SparseCore 0:
  270.8 16.5 all-gather.2

commit v5 on v2

--- a/solution.py
+++ b/solution.py
@@ -66,7 +66,7 @@
             ],
         ),
         out_shape=jax.ShapeDtypeStruct((pair_count, width, width), jnp.bfloat16),
-        compiler_params=pltpu.CompilerParams(vmem_limit_bytes=32 << 20),
+        compiler_params=pltpu.CompilerParams(vmem_limit_bytes=56 << 20),
         cost_estimate=pl.CostEstimate(
             flops=2 * pair_count * slot_count * tile_rows * width * width,
             bytes_accessed=4 * pair_count * slot_count * tile_rows * width,
@@ -104,11 +104,13 @@
 
 
 def last_gamma_kernel(
-    orb_ref, match_ref, source_ref, weight_ref, start_ref, out_ref, rows_ref, total_ref
+    orb_ref, match_ref, source_ref, weight_ref, start_ref, out_ref, rows_ref, total_ref, sem
 ):
     @pl.when(pl.program_id(0) == 0)
     def _():
-        total_ref[...] = start_ref[...]
+        load = pltpu.make_async_copy(start_ref, total_ref, sem)
+        load.start()
+        load.wait()
 
     add_terms(orb_ref, match_ref, source_ref, weight_ref, total_ref, rows_ref)
 
@@ -133,8 +135,8 @@
         body, out_type = first_gamma_kernel, jnp.float32
     else:
         body, out_type = last_gamma_kernel, jnp.bfloat16
-        in_specs.append(whole)
-        scratch.append(pltpu.VMEM(total_shape, jnp.float32))
+        in_specs.append(pl.BlockSpec(memory_space=pl.ANY))
+        scratch += [pltpu.VMEM(total_shape, jnp.float32), pltpu.SemaphoreType.DMA]
         operands.append(start)
     return pl.pallas_call(
         body,
@@ -146,7 +148,7 @@
             scratch_shapes=scratch,
         ),
         out_shape=jax.ShapeDtypeStruct(total_shape, out_type),
-        compiler_params=pltpu.CompilerParams(vmem_limit_bytes=48 << 20),
+        compiler_params=pltpu.CompilerParams(vmem_limit_bytes=56 << 20),
         cost_estimate=pl.CostEstimate(
             flops=2 * term_count * slot_count * tile_rows * width * width,
             bytes_accessed=2 * term_count * slot_count * tile_rows * width
@@ -164,15 +166,6 @@
         block = lax.dynamic_index_in_dim(blocks, lax.rem(me + shift, count), 0, keepdims=False)
         arrived.append(lax.ppermute(block, axis, [(d, (d + shift) % count) for d in range(count)]))
     return arrived
-
-
-def sum_everywhere(block, axis):
-    count = lax.axis_size(axis)
-    total = block.astype(jnp.float32)
-    for shift in range(1, count):
-        moved = lax.ppermute(block, axis, [(d, (d + shift) % count) for d in range(count)])
-        total = total + moved.astype(jnp.float32)
-    return total
 
 
 def pair_weights(partial, energy_pair, vir_energy):
@@ -265,7 +258,11 @@
     density = parts[0].astype(jnp.float32)
     for part in parts[1:]:
         density = density + part.astype(jnp.float32)
-    density = sum_everywhere(density.astype(jnp.bfloat16), "occ")
+    density = density + lax.ppermute(density.astype(jnp.bfloat16), "occ", swapped).astype(jnp.float32)
+    block = density.astype(jnp.bfloat16)
+    for shift in range(1, half):
+        turned = [(d, d // half * half + (d + shift) % half) for d in range(peer_count)]
+        density = density + lax.ppermute(block, "occ", turned).astype(jnp.float32)
 
     gamma = gamma_call(own, far_match, far_tiles, weights, gamma, orb_count)
     return gamma, density

time: 396 us -> 393 us (level)
  starting transfers between devices: 32.9 us -> 27.4 us
  Pallas kernels: 57.5 us -> 61.8 us
    unnamed x18 -> x10, local copies, waits for them, and re-layouts: 8.98 us -> 2.15 us
    ppermute x7 -> x4, starting transfers between devices: 12.5 us -> 7.05 us  [the longest x3 4.2 us: per_device(): density = density + lax.ppermute(block, 'occ', turned).astype(jnp.float32)]
  transfers between devices with their start and end apart: 21 -> 18, of which waited for: 13 -> 14; matrix products, arithmetic and copies ran while one was open for 6% -> 7% of each run, Pallas kernels for 7% -> 8%
where the time goes in v5:
time: 393 us; the launch traced here: 392 us
  waiting for transfers between devices  232 us (59%)
  Pallas kernels  61.8 us (16%)
  local copies, waits for them, and re-layouts  34.3 us (9%)
  starting transfers between devices  27.4 us (7%)
  between operations  15 us (4%)
  blocking collectives  13.1 us (3%)
  other arithmetic  6.4 us (2%)
    ppermute x1, waiting for transfers between devices, per_device(): partner_tiles = lax.ppermute(own_tiles, 'occ', swapped)  179 us
    pallas_call x2, Pallas kernels, gamma_call(): pl.pallas_call(body, grid_spec=pltpu.PrefetchScalarGridSpec(num_scalar_pr...  32.7 us
    pallas_call x2, Pallas kernels, coulomb_call(): pl.pallas_call(coulomb_kernel, grid_spec=pltpu.PrefetchScalarGridSpec(num...  29.2 us
    ppermute x9, waiting for transfers between devices, exchange(): lax.ppermute(block, axis, [(d, (d + shift) % count) for d in range(count)])  21.4 us
    all_gather x2, waiting for transfers between devices, pair_weights(): lax.all_gather(mixed.astype(jnp.bfloat16), 'aux', axis=0, tiled=True)  15.5 us
    gather x2, local copies, waits for them, and re-layouts, near_exchange(): tiles[wanted_of(owner)]  13.7 us
    unnamed x1, blocking collectives  13.1 us
    all_to_all x2, waiting for transfers between devices, near_exchange(): lax.all_to_all(tiles[wanted_of(owner)], 'occ', split_axis=0, concat_axis=...  11.8 us
  transfers between devices with their start and end apart: 18, of which 14 were waited for; matrix products, arithmetic and copies ran while one was open for 7% of the time, Pallas kernels for 8%

profile of v5, /device:TPU:0, one launch (start us, length us, event | category | flops | bytes accessed | tf_op | source)
XLA Modules:
  0.0 391.5 jit_solution(14993788161924901944)
XLA Ops:
  7.2 0.8 fusion.13
  8.0 0.8 copy.56
  8.9 1.2 dynamic-slice
  11.0 13.1 %all-reduce = s32[640]{0:T(1024)S(1)} all-reduce(s32[640]{0:T(1024)S(1)} %add_dynamic-update-slice_fusion), channel_id=2, replica_groups=mesh['occ'=8,'aux'=4] {'occ'}, use_global_device_ids=true, to_apply=%add | all-reduce | flops 640 | bytes 5120
  24.9 0.7 gather_fusion.10
  25.7 6.8 %gather_fusion.15 = bf16[8,16,128,256]{3,2,1,0:T(8,128)(2,1)} fusion(bf16[4,16,128,256]{3,2,1,0:T(8,128)(2,1)} %right_ref.3, s32[1024]{0:T(1024)S(1)} %pad_clamp_fusion.2), kind=kCustom, calls=%fused_computation.15 | custom fusion | bytes 16777248 | tf_op jit(solution)/shard_map/gather | solution.py:233
  32.5 5.6 %all-to-all-start.1 = ((bf16[8,16,128,256]{3,2,1,0:T(8,128)(2,1)}), bf16[8,16,128,256]{3,2,1,0:T(8,128)(2,1)}, u32[]{:S(2)}, u32[]{:S(2)}) async-start(bf16[8,16,128,256]{3,2,1,0:T(8,128)(2,1)} %gather_fusion.15), calls=%async_computation.1 | async-start | bytes 16777216 | tf_op jit(solution)/shard_map/all_to_all | solution.py:232
  39.2 0.7 gather_fusion.7
  40.1 178.7 %collective-permute-done = bf16[4,16,128,256]{3,2,1,0:T(8,128)(2,1)} collective-permute-done((bf16[4,16,128,256]{3,2,1,0:T(8,128)(2,1)}, bf16[4,16,128,256]{3,2,1,0:T(8,128)(2,1)}, u32[]{:S(2)}, u32[]{:S(2)}) %collective-permute-start) | collective-permute-done | bytes 4194336 | tf_op jit(solution)/shard_map/ppermute | solution.py:242
  218.8 6.9 %gather_fusion.8 = bf16[8,16,128,256]{3,2,1,0:T(8,128)(2,1)} fusion(bf16[4,16,128,256]{3,2,1,0:T(8,128)(2,1)} %collective-permute-done, s32[1024]{0:T(1024)S(1)} %pad_clamp_fusion.5), kind=kCustom, calls=%fused_computation.8 | custom fusion | bytes 16777248 | tf_op jit(solution)/shard_map/gather | solution.py:233
  225.7 5.7 %all-to-all-start = ((bf16[8,16,128,256]{3,2,1,0:T(8,128)(2,1)}), bf16[8,16,128,256]{3,2,1,0:T(8,128)(2,1)}, u32[]{:S(2)}, u32[]{:S(2)}) async-start(bf16[8,16,128,256]{3,2,1,0:T(8,128)(2,1)} %gather_fusion.8), calls=%async_computation | async-start | bytes 16777216 | tf_op jit(solution)/shard_map/all_to_all | solution.py:232
  232.9 0.7 gather_fusion.13
  234.5 0.7 gather_fusion.4
  239.1 0.7 gather_fusion.1
  242.0 1.0 select_reduce_fusion.1
  243.1 14.5 %shard_map.77 = bf16[8,256,256]{2,1,0:T(8,128)(2,1)} custom-call(s32[8]{0:T(128)} %reshape.420.orb_ref, s32[8,16]{1,0:T(8,128)} %get-tuple-element.12.match_ref, bf16[8,16,128,256]{3,2,1,0:T(8,128)(2,1)} %all-to-all-done.1.left_ref.source_ref, bf16[4,16,128,256]{3,2,1,0:T(8,128)(2,1)} %right_ref.3), custom_call_target="tpu_custom_call" | custom-call | flops 2147483648 | bytes 16777216 | tf_op jit(solution)/shard_map/pallas_call | solution.py:53
  257.6 1.3 constant_dynamic-slice_fusion.3
  259.2 1.6 collective-permute-start.2
  260.9 1.5 collective-permute-start.3
  263.0 3.9 collective-permute-done.1
  266.9 1.5 collective-permute-done.2
  268.4 3.9 collective-permute-done.3
  272.7 0.8 fusion.33
  274.2 1.0 select_reduce_fusion
  275.2 15.5 %all-gather.4.cloned.1.call-done.weight_ref = bf16[8,256,256]{2,1,0:T(8,128)(2,1)} async-done(((bf16[2,256,256]{2,1,0:T(8,128)(2,1)}), bf16[8,256,256]{2,1,0:T(8,128)(2,1)}) %all-gather.4.cloned.1.call-update) | async-done | bytes 1048592 | tf_op jit(solution)/shard_map/all_gather | solution.py:184
  290.7 15.2 %shard_map.78.start_ref = f32[4,16,128,256]{3,2,1,0:T(8,128)} custom-call(s32[8]{0:T(128)} %reshape.420.orb_ref, s32[8,16]{1,0:T(8,128)} %get-tuple-element.13.match_ref, bf16[8,16,128,256]{3,2,1,0:T(8,128)(2,1)} %all-to-all-done.1.left_ref.source_ref, bf16[8,256,256]{2,1,0:T(8,128)(2,1)} %all-gather.4.cloned.1.call-done.weight_ref), custom_call_target="tpu_custom_call" | custom-call | flops 2147483648 | bytes 25165824 | tf_op jit(solution)/shard_map/pallas_call | solution.py:141
  306.0 11.8 %all-to-all-done.left_ref.source_ref = bf16[8,16,128,256]{3,2,1,0:T(8,128)(2,1)} async-done(((bf16[8,16,128,256]{3,2,1,0:T(8,128)(2,1)}), bf16[8,16,128,256]{3,2,1,0:T(8,128)(2,1)}, u32[]{:S(2)}, u32[]{:S(2)}) %all-to-all-start) | async-done | bytes 8388640 | tf_op jit(solution)/shard_map/all_to_all | solution.py:232
  317.7 14.6 %shard_map.79 = bf16[8,256,256]{2,1,0:T(8,128)(2,1)} custom-call(s32[8]{0:T(128)} %reshape.416.orb_ref, s32[8,16]{1,0:T(8,128)} %get-tuple-element.10.match_ref, bf16[8,16,128,256]{3,2,1,0:T(8,128)(2,1)} %all-to-all-done.left_ref.source_ref, bf16[4,16,128,256]{3,2,1,0:T(8,128)(2,1)} %right_ref.3), custom_call_target="tpu_custom_call" | custom-call | flops 2147483648 | bytes 16777216 | tf_op jit(solution)/shard_map/pallas_call | solution.py:53
  332.4 1.2 dynamic-slice_bitcast_fusion.2
  333.6 1.6 collective-permute-start.5
  335.2 1.4 collective-permute-start.6
  337.1 4.4 %collective-permute-done.4 = bf16[2,256,256]{2,1,0:T(8,128)(2,1)S(1)} collective-permute-done((bf16[2,256,256]{2,1,0:T(8,128)(2,1)S(1)}, bf16[2,256,256]{2,1,0:T(8,128)(2,1)S(1)}, u32[]{:S(2)}, u32[]{:S(2)}) %collective-permute-start.4) | collective-permute-done | bytes 262176 | tf_op jit(solution)/shard_map/ppermute | solution.py:167
  341.6 1.2 collective-permute-done.5
  342.8 4.0 %collective-permute-done.6 = bf16[2,256,256]{2,1,0:T(8,128)(2,1)S(1)} collective-permute-done((bf16[2,256,256]{2,1,0:T(8,128)(2,1)S(1)}, bf16[2,256,256]{2,1,0:T(8,128)(2,1)S(1)}, u32[]{:S(2)}, u32[]{:S(2)}) %collective-permute-start.6) | collective-permute-done | bytes 262176 | tf_op jit(solution)/shard_map/ppermute | solution.py:167
  346.8 1.1 fusion.4
  348.3 0.8 copy.73
  350.5 0.8 collective-permute-start.7
  351.4 1.5 collective-permute-start.8
  352.9 1.2 collective-permute-done.7
  354.1 1.2 collective-permute-done.8
  355.3 2.8 collective-permute-start.10
  358.2 2.3 collective-permute-done.10
  360.5 2.2 collective-permute-start.11
  362.6 2.0 collective-permute-start.13
  364.7 1.0 collective-permute-done.11
  365.7 0.8 collective-permute-done.12
  366.5 0.7 convert_add_fusion.3
  367.2 17.5 %shard_map.80 = bf16[4,16,128,256]{3,2,1,0:T(8,128)(2,1)} custom-call(s32[8]{0:T(128)} %reshape.416.orb_ref, s32[8,16]{1,0:T(8,128)} %get-tuple-element.11.match_ref, bf16[8,16,128,256]{3,2,1,0:T(8,128)(2,1)} %all-to-all-done.left_ref.source_ref, bf16[8,256,256]{2,1,0:T(8,128)(2,1)} %all-gather.6.cloned.1.call-done.weight_ref, ...), custom_call_target="tpu_custom_call" | custom-call | flops 2147483648 | bytes 25165824 | tf_op jit(solution)/shard_map/pallas_call | solution.py:141
  (109 shorter events, 15.6 us)
Async XLA Ops:
  7.2 229.4 %copy-start = (f32[32]{0:T(128)S(1)}, f32[32]{0:T(128)}, u32[]{:S(2)}) copy-start(f32[32]{0:T(128)} %param.10) | copy-start | bytes 388
  32.5 193.2 %all-to-all-start.1 = ((bf16[8,16,128,256]{3,2,1,0:T(8,128)(2,1)}), bf16[8,16,128,256]{3,2,1,0:T(8,128)(2,1)}, u32[]{:S(2)}, u32[]{:S(2)}) async-start(bf16[8,16,128,256]{3,2,1,0:T(8,128)(2,1)} %gather_fusion.15), calls=%async_computation.1 | async-start | bytes 16777216 | tf_op jit(solution)/shard_map/all_to_all | solution.py:232
  38.1 180.6 %collective-permute-start = (bf16[4,16,128,256]{3,2,1,0:T(8,128)(2,1)}, bf16[4,16,128,256]{3,2,1,0:T(8,128)(2,1)}, u32[]{:S(2)}, u32[]{:S(2)}) collective-permute-start(bf16[4,16,128,256]{3,2,1,0:T(8,128)(2,1)} %right_ref.3), channel_id=1, source_target_pairs={{0,16},{4,20},{8,24},{12,28},{16,0},{20,4},{24,8},{28,12},{1,17},{... | collective-permute-start | bytes 12582920 | tf_op jit(solution)/shard_map/ppermute | solution.py:242
  225.7 92.0 %all-to-all-start = ((bf16[8,16,128,256]{3,2,1,0:T(8,128)(2,1)}), bf16[8,16,128,256]{3,2,1,0:T(8,128)(2,1)}, u32[]{:S(2)}, u32[]{:S(2)}) async-start(bf16[8,16,128,256]{3,2,1,0:T(8,128)(2,1)} %gather_fusion.8), calls=%async_computation | async-start | bytes 16777216 | tf_op jit(solution)/shard_map/all_to_all | solution.py:232
  231.4 59.3 %all-gather.4.cloned.1.call-start = ((), (), s32[]{:S(2)}) async-start(), calls=%async_computation.2 | async-start | bytes 1310720 | tf_op jit(solution)/shard_map/all_gather | solution.py:184
  243.1 19.4 %copy-start.2 = (f32[256]{0:T(256)S(1)}, f32[256]{0:T(256)}, u32[]{:S(2)}) copy-start(f32[256]{0:T(256)} %param.11) | copy-start | bytes 3076
  259.0 7.9 %collective-permute-start.1 = (bf16[2,256,256]{1,2,0:T(8,128)(2,1)S(1)}, bf16[2,256,256]{1,2,0:T(8,128)(2,1)S(1)}, u32[]{:S(2)}, u32[]{:S(2)}) collective-permute-start(bf16[2,256,256]{1,2,0:T(8,128)(2,1)S(1)} %bitcast.116), channel_id=1, source_target_pairs={{0,1},{1,2},{2,3},{3,0},{4,5},{5,6},{6,7},{7,4},{8,9},{9,10},{10,1... | collective-permute-start | bytes 786440 | tf_op jit(solution)/shard_map/ppermute | solution.py:167
  259.2 9.2 %collective-permute-start.2 = (bf16[2,256,256]{1,2,0:T(8,128)(2,1)S(1)}, bf16[2,256,256]{1,2,0:T(8,128)(2,1)S(1)}, u32[]{:S(2)}, u32[]{:S(2)}) collective-permute-start(bf16[2,256,256]{1,2,0:T(8,128)(2,1)S(1)} %bitcast.117), channel_id=1, source_target_pairs={{0,2},{1,3},{2,0},{3,1},{4,6},{5,7},{6,4},{7,5},{8,10},{9,11},{10,... | collective-permute-start | bytes 786440 | tf_op jit(solution)/shard_map/ppermute | solution.py:167
  260.9 11.4 %collective-permute-start.3 = (bf16[2,256,256]{1,2,0:T(8,128)(2,1)S(1)}, bf16[2,256,256]{1,2,0:T(8,128)(2,1)S(1)}, u32[]{:S(2)}, u32[]{:S(2)}) collective-permute-start(bf16[2,256,256]{1,2,0:T(8,128)(2,1)S(1)} %bitcast.118), channel_id=1, source_target_pairs={{0,3},{1,0},{2,1},{3,2},{4,7},{5,4},{6,5},{7,6},{8,11},{9,8},{10,9... | collective-permute-start | bytes 786440 | tf_op jit(solution)/shard_map/ppermute | solution.py:167
  273.5 93.7 %all-gather.6.cloned.1.call-start = ((), (), s32[]{:S(2)}) async-start(), calls=%async_computation.3 | async-start | bytes 1310720 | tf_op jit(solution)/shard_map/all_gather | solution.py:184
  333.5 8.0 %collective-permute-start.4 = (bf16[2,256,256]{2,1,0:T(8,128)(2,1)S(1)}, bf16[2,256,256]{2,1,0:T(8,128)(2,1)S(1)}, u32[]{:S(2)}, u32[]{:S(2)}) collective-permute-start(bf16[2,256,256]{2,1,0:T(8,128)(2,1)S(1)} %get-tuple-element.22), channel_id=1, source_target_pairs={{0,1},{1,2},{2,3},{3,0},{4,5},{5,6},{6,7},{7,4},{8,9},{9,10},{10,1... | collective-permute-start | bytes 786440 | tf_op jit(solution)/shard_map/ppermute | solution.py:167
  333.6 9.2 %collective-permute-start.5 = (bf16[2,256,256]{2,1,0:T(8,128)(2,1)S(1)}, bf16[2,256,256]{2,1,0:T(8,128)(2,1)S(1)}, u32[]{:S(2)}, u32[]{:S(2)}) collective-permute-start(bf16[2,256,256]{2,1,0:T(8,128)(2,1)S(1)} %get-tuple-element.24), channel_id=1, source_target_pairs={{0,2},{1,3},{2,0},{3,1},{4,6},{5,7},{6,4},{7,5},{8,10},{9,11},{10,... | collective-permute-start | bytes 786440 | tf_op jit(solution)/shard_map/ppermute | solution.py:167
  335.2 11.7 %collective-permute-start.6 = (bf16[2,256,256]{2,1,0:T(8,128)(2,1)S(1)}, bf16[2,256,256]{2,1,0:T(8,128)(2,1)S(1)}, u32[]{:S(2)}, u32[]{:S(2)}) collective-permute-start(bf16[2,256,256]{2,1,0:T(8,128)(2,1)S(1)} %get-tuple-element.23), channel_id=1, source_target_pairs={{0,3},{1,0},{2,1},{3,2},{4,7},{5,4},{6,5},{7,6},{8,11},{9,8},{10,9... | collective-permute-start | bytes 786440 | tf_op jit(solution)/shard_map/ppermute | solution.py:167
  350.5 3.6 collective-permute-start.7
  351.4 3.9 collective-permute-start.8
  352.9 2.4 collective-permute-start.9
  355.3 5.1 %collective-permute-start.10 = (bf16[64,256]{1,0:T(8,128)(2,1)S(1)}, bf16[64,256]{1,0:T(8,128)(2,1)S(1)}, u32[]{:S(2)}, u32[]{:S(2)}) collective-permute-start(bf16[64,256]{1,0:T(8,128)(2,1)S(1)} %get-tuple-element.14), channel_id=1, source_target_pairs={{0,16},{4,20},{8,24},{12,28},{16,0},{20,4},{24,8},{28,12},{1,17},{... | collective-permute-start | bytes 98312 | tf_op jit(solution)/shard_map/ppermute | solution.py:261
  360.5 5.3 %collective-permute-start.11 = (bf16[64,256]{1,0:T(8,128)(2,1)S(1)}, bf16[64,256]{1,0:T(8,128)(2,1)S(1)}, u32[]{:S(2)}, u32[]{:S(2)}) collective-permute-start(bf16[64,256]{1,0:T(8,128)(2,1)S(1)} %fusion.12), channel_id=1, source_target_pairs={{0,4},{4,8},{8,12},{12,0},{16,20},{20,24},{24,28},{28,16},{1,5},{5... | collective-permute-start | bytes 98312 | tf_op jit(solution)/shard_map/ppermute | solution.py:265
  362.6 3.9 collective-permute-start.12
  362.6 3.9 collective-permute-start.13
  367.2 17.5 %copy-start.1 = (f32[32]{0:T(128)S(1)}, f32[32]{0:T(128)}, u32[]{:S(2)}) copy-start(f32[32]{0:T(128)} %param.10) | copy-start | bytes 388
Sparse Core Ops, SparseCore 0:
  273.6 17.0 all-gather.3
  349.3 17.5 all-gather.5
